TPU v7x, 128 devices: a whole 4x4x4 slice. The times are simulated.
128 devices in a mesh: row: 8 (over y_lo, z), col: 16 (over x, y_hi, core).
Axes of the slice: x: 4, y: 4 (y_hi: 2, y_lo: 2; y = y_hi * 2 + y_lo), z: 4, core: 2. Of those that a mesh axis runs over, the one named last changes fastest.
Arguments:
- queries: bfloat16 [16384, 512], P(('row', 'col')), may hold values from -6 to 6
- keys: bfloat16 [16384, 512], P(('row', 'col')), may hold values from -6 to 6
- fwd_table: bfloat16 [256, 16384], P(('row', 'col')), may hold values from 0.0099487305 to 1
- bwd_table: bfloat16 [256, 16384], P(('row', 'col')), may hold values from 0.0099487305 to 1
- step_weight: float32 [256], P(('row', 'col')), may hold values from 1000 to 6000
- block_order: int32 [512], replicated, may hold values from 0 to 511, each once
Outputs:
- query_grad: float32 [16384, 512], P(('row', 'col'))
- key_grad: float32 [16384, 512], P(('row', 'col'))
Inputs may be any that keep to these rules, and one draw needn't show every extreme that they name: `block_order`: each value occurs exactly once.
All inputs are finite; a program needn't handle non-finite values.
Results may differ from a plain program's by a relative error of at most 0.01.
Values may be sent and summed in bfloat16 or wider, within the bound.
A program may use at most 192 MiB of HBM per device.

v0:
```python
import jax
import jax.numpy as jnp
from jax import lax
from jax.sharding import PartitionSpec as P

HEADS = 8
HEAD = 64
GRAIN = 32


NEG = -1e30


def combined_all(part, axis, combine):
    gathered = jax.tree.map(lambda a: lax.all_gather(a, axis), part)

    def take(source):
        return jax.tree.map(lambda a: lax.dynamic_index_in_dim(a, source, 0, False), gathered)

    return lax.fori_loop(
        1, lax.axis_size(axis), lambda source, state: combine(state, take(source)), take(0)
    )


def slot_positions(grains):
    offsets = jnp.arange(GRAIN, dtype=jnp.int32)
    return ((grains * GRAIN)[:, None] + offsets[None, :]).reshape(grains.shape[0] * GRAIN)


def combine_stats(earlier, later):
    top = jnp.maximum(earlier[0], later[0])
    left = jnp.exp(earlier[0] - top)
    right = jnp.exp(later[0] - top)
    return (top, earlier[1] * left + later[1] * right, earlier[2] * left + later[2] * right)


def head_scores(src_q, tgt_k, head, valid, scale):
    q_part = src_q[:, head * HEAD : (head + 1) * HEAD]
    k_part = tgt_k[:, head * HEAD : (head + 1) * HEAD]
    raw = (
        lax.dot_general(
            q_part, k_part, (((1,), (1,)), ((), ())), preferred_element_type=jnp.float32
        )
        * scale
    )
    return jnp.where(valid, raw, NEG)


def local_stats(src_q, tgt_k, counts, valid, scale):
    kept = []
    tops = []
    totals = []
    sums = []
    for head in range(HEADS):
        scores = head_scores(src_q, tgt_k, head, valid, scale)
        top = jnp.max(scores, axis=1)
        weights = jnp.where(valid, jnp.exp(scores - top[:, None]), 0.0)
        tops.append(top)
        totals.append(jnp.sum(weights, axis=1))
        sums.append(jnp.sum(weights * counts, axis=1))
    return (kept, (jnp.stack(tops), jnp.stack(totals), jnp.stack(sums)))


def grad_terms(src_q, tgt_k, counts, valid, scale, merged):
    top_all, total_all, expected_all = merged
    q_terms = []
    k_terms = []
    for head in range(HEADS):
        scores = head_scores(src_q, tgt_k, head, valid, scale)
        weights = jnp.where(valid, jnp.exp(scores - top_all[head][:, None]), 0.0)
        total = total_all[head][:, None]
        grad = (weights / total * (expected_all[head][:, None] / total - counts) / HEADS).astype(
            jnp.bfloat16
        )
        k_part = tgt_k[:, head * HEAD : (head + 1) * HEAD]
        q_part = src_q[:, head * HEAD : (head + 1) * HEAD]
        q_terms.append(jnp.dot(grad, k_part, preferred_element_type=jnp.float32) * scale)
        k_terms.append(
            lax.dot_general(
                grad, q_part, (((0,), (0,)), ((), ())), preferred_element_type=jnp.float32
            )
            * scale
        )
    return (jnp.concatenate(q_terms, axis=1), jnp.concatenate(k_terms, axis=1))


def local(queries, keys, fwd_table, bwd_table, step_weight, block_order):
    n_row = lax.axis_size("row")
    n_col = lax.axis_size("col")
    row_id = lax.axis_index("row")
    col_id = lax.axis_index("col")
    tile = queries.shape[0]
    scale = HEAD ** (-0.5)
    scaled = (bwd_table.astype(jnp.float32) * step_weight[:, None]).astype(jnp.bfloat16)
    own_fwd, own_bwd = (
        lax.all_to_all(fwd_table, ("row", "col"), split_axis=1, concat_axis=0, tiled=True),
        lax.all_to_all(scaled, ("row", "col"), split_axis=1, concat_axis=0, tiled=True),
    )
    grain_grid = block_order.reshape(n_row, n_col, tile // GRAIN)
    line_grains = lax.dynamic_index_in_dim(grain_grid, row_id, 0, keepdims=False).reshape(
        n_col * (tile // GRAIN)
    )
    column_grains = lax.dynamic_index_in_dim(grain_grid, col_id, 1, keepdims=False).reshape(
        n_row * (tile // GRAIN)
    )
    src_q, src_fwd = (
        lax.all_gather(queries, "col", axis=0, tiled=True),
        lax.all_gather(own_fwd, "col", axis=1, tiled=True),
    )
    tgt_k, tgt_bwd = (
        lax.all_gather(keys, "row", axis=0, tiled=True),
        lax.all_gather(own_bwd, "row", axis=1, tiled=True),
    )
    valid = slot_positions(line_grains)[:, None] <= slot_positions(column_grains)[None, :]
    counts = lax.dot_general(
        src_fwd, tgt_bwd, (((0,), (0,)), ((), ())), preferred_element_type=jnp.float32
    )
    kept, partial_value = local_stats(src_q, tgt_k, counts, valid, scale)
    merged = combined_all(partial_value, "col", combine_stats)
    q_total, k_total = grad_terms(src_q, tgt_k, counts, valid, scale, merged)
    query_grad = lax.psum_scatter(q_total, "col", scatter_dimension=0, tiled=True)
    key_grad = lax.psum_scatter(
        k_total.astype(jnp.bfloat16), "row", scatter_dimension=0, tiled=True
    ).astype(jnp.float32)
    return (query_grad, key_grad)


def solution(mesh):
    return jax.shard_map(
        local,
        mesh=mesh,
        in_specs=(
            P(("row", "col"), None),
            P(("row", "col"), None),
            P(("row", "col"), None),
            P(("row", "col"), None),
            P(("row", "col")),
            P(),
        ),
        out_specs=(P(("row", "col"), None), P(("row", "col"), None)),
        check_vma=False,
    )
```

profile of v0, /device:TPU:1, one launch (start us, length us, event | category | flops | bytes accessed | tf_op | source)
XLA Modules:
  0.0 511.9 jit_solution(8629273392706704662)
XLA Ops:
  8.6 1.6 fusion.107
  10.2 11.5 %all-to-all-start = ((bf16[2,128,128]{2,0,1:T(2,128)(2,1)}), bf16[2,128,128]{2,0,1:T(2,128)(2,1)S(1)}, u32[]{:S(2)}, u32[]{:S(2)}) async-start(bf16[2,128,128]{2,0,1:T(2,128)(2,1)} %fusion.107), calls=%async_computation | async-start | bytes 131072 | tf_op jit(solution)/shard_map/all_to_all | solution.py:97
  23.1 8.2 %all-to-all-done = bf16[2,128,128]{2,0,1:T(2,128)(2,1)S(1)} async-done(((bf16[2,128,128]{2,0,1:T(2,128)(2,1)}), bf16[2,128,128]{2,0,1:T(2,128)(2,1)S(1)}, u32[]{:S(2)}, u32[]{:S(2)}) %all-to-all-start) | async-done | bytes 65568 | tf_op jit(solution)/shard_map/all_to_all | solution.py:97
  31.3 4.0 all-to-all-start.1
  35.4 25.2 %all_gather.36 = bf16[256,1024]{1,0:T(8,128)(2,1)} all-gather(bf16[256,128]{1,0:T(8,128)(2,1)S(1)} %bitcast.169), channel_id=1, replica_groups=mesh['row'=8,'col'=16] {'row'}, dimensions={1}, use_global_device_ids=true | all-gather | bytes 589824 | tf_op jit(solution)/shard_map/all_gather | solution.py:112
  61.3 41.2 %all-gather.10.cloned.1.call-done = bf16[2048,512]{1,0:T(8,128)(2,1)} async-done(((bf16[128,512]{1,0:T(8,128)(2,1)}), bf16[2048,512]{1,0:T(8,128)(2,1)}) %all-gather.10.cloned.1.call-update) | async-done | bytes 2097168 | tf_op jit(solution)/shard_map/all_gather | solution.py:107
  102.5 5.7 %fusion.113 = (f32[2048]{0:T(1024)S(1)}, f32[2048,1024]{0,1:T(8,128)}) fusion(bf16[1024,512]{1,0:T(8,128)(2,1)} %all-gather.12.cloned.1.call-done, bf16[2048,512]{1,0:T(8,128)(2,1)} %all-gather.10.cloned.1.call-done, s32[1024]{0:T(1024)S(1)} %add.120, s32[2048]{0:T(1024)S(1)} %add.115), kind=kOutput, calls=%fused_computation.179 | convolution fusion | flops 276822016 | bytes 9195520 | tf_op jit(solution)/shard_map/dot_general | solution.py:41
  108.3 4.1 fusion.112
  112.4 4.1 fusion.118
  116.5 4.1 fusion.114
  120.6 4.0 fusion.115
  124.6 4.1 fusion.116
  128.6 4.0 fusion.117
  132.6 3.9 fusion.111
  137.6 12.0 %all-gather.14.cloned.1.call-done = bf16[256,2048]{1,0:T(8,128)(2,1)} async-done(((bf16[256,128]{1,0:T(8,128)(2,1)}), bf16[256,2048]{1,0:T(8,128)(2,1)}) %all-gather.14.cloned.1.call-update) | async-done | bytes 1048592 | tf_op jit(solution)/shard_map/all_gather | solution.py:108
  149.6 32.4 %fusion.34 = (f32[2048]{0:T(1024)S(1)}, f32[2048]{0:T(1024)S(1)}, f32[2048]{0:T(1024)S(1)}, f32[2048]{0:T(1024)S(1)}, f32[2048]{0:T(1024)S(1)}, /*index=5*/f32[2...) fusion(f32[2048,1024]{0,1:T(8,128)} %get-tuple-element.282, ...), kind=kOutput, calls=%fused_computation.79 | convolution fusion | flops 1159692288 | bytes 77279232 | tf_op jit(solution)/shard_map/dot_general | solution.py:115
  183.6 12.4 %all-gather.16.cloned.1.call-done = f32[128,2048]{1,0:T(8,128)} async-done(((f32[8,2048]{1,0:T(8,128)}), f32[128,2048]{1,0:T(8,128)}) %all-gather.16.cloned.1.call-update) | async-done | bytes 1048592 | tf_op jit(solution)/shard_map/all_gather | solution.py:15
  196.8 45.0 %all-gather.20.cloned.1.call-done = f32[128,2048]{1,0:T(8,128)} async-done(((f32[8,2048]{1,0:T(8,128)}), f32[128,2048]{1,0:T(8,128)}) %all-gather.20.cloned.1.call-update) | async-done | bytes 1048592 | tf_op jit(solution)/shard_map/all_gather | solution.py:15
  242.7 45.6 %all-gather.18.cloned.1.call-done = f32[128,2048]{1,0:T(8,128)} async-done(((f32[8,2048]{1,0:T(8,128)}), f32[128,2048]{1,0:T(8,128)}) %all-gather.18.cloned.1.call-update) | async-done | bytes 1048592 | tf_op jit(solution)/shard_map/all_gather | solution.py:15
  289.1 28.2 %while.19 = (s32[]{:T(128)}, f32[8,2048]{1,0:T(8,128)S(1)}, f32[8,2048]{1,0:T(8,128)S(1)}, f32[8,2048]{1,0:T(8,128)S(1)}, f32[16,8,2048]{2,1,0:T(8,128)}, /*inde...) while((s32[]{:T(128)}, f32[8,2048]{1,0:T(8,128)S(1)}, ...), condition=%wide.region_25.26_spmd, body=%wide.region_24.25_spmd.sunk | while | flops 180229 | bytes 917647 | solution.py:20
  290.0 0.9 fusion.140
  291.0 0.9 fusion.139
  291.9 0.9 fusion.140
  292.9 0.9 fusion.139
  293.8 0.9 fusion.140
  294.8 0.9 fusion.139
  295.7 0.9 fusion.140
  296.6 0.9 fusion.139
  297.6 0.9 fusion.140
  298.5 0.9 fusion.139
  299.4 0.9 fusion.140
  300.4 0.9 fusion.139
  301.3 0.9 fusion.140
  303.2 0.9 fusion.140
  305.1 0.9 fusion.140
  307.0 0.9 fusion.140
  308.8 0.9 fusion.140
  310.7 0.9 fusion.140
  312.6 0.9 fusion.140
  314.5 0.9 fusion.140
  316.4 0.9 fusion.140
  320.5 16.7 %fusion.35 = (bf16[2048,1024]{0,1:T(8,128)(2,1)S(1)}, bf16[2048,1024]{0,1:T(8,128)(2,1)S(1)}, bf16[2048,1024]{0,1:T(8,128)(2,1)S(1)}, bf16[2048,1024]{0,1:T(8,128)(2,1)S(1)}) fusion(f32[1024,2048]{1,0:T(8,128)} %get-tuple-element.283, f32[2048,1024]{0,1:T(8,128)} %get-tuple-element.282, f32[2048]{0:T(1024)S(1)} %div.206, f32[2048]{0:T(1024)S(1)} %bitcast.188, ...), kind=kLoop, calls=%fused_computation.80 | loop fusion | flops 60817408 | bytes 58830848 | tf_op jit(solution)/shard_map/convert_element_type | solution.py:72
  337.3 26.8 %fusion.36 = (bf16[2048,1024]{0,1:T(8,128)(2,1)S(1)}, bf16[2048,1024]{0,1:T(8,128)(2,1)}, bf16[2048,1024]{0,1:T(8,128)(2,1)}, bf16[2048,1024]{0,1:T(8,128)(2,1)}) fusion(f32[1024,2048]{1,0:T(8,128)} %get-tuple-element.283, f32[2048,1024]{0,1:T(8,128)} %get-tuple-element.280, f32[2048]{0:T(1024)} %div.201, f32[2048]{0:T(1024)S(1)} %bitcast.180, ...), kind=kLoop, calls=%fused_computation.81 | loop fusion | flops 60817408 | bytes 58830848 | tf_op jit(solution)/shard_map/convert_element_type | solution.py:72
  364.1 2.0 fusion.60
  366.2 2.1 fusion.62
  368.3 2.1 fusion.64
  370.3 2.1 fusion.66
  372.5 2.1 fusion.68
  374.5 2.1 fusion.70
  376.7 2.1 fusion.72
  378.7 2.1 fusion.74
  380.8 2.4 copy.18
  383.5 4.0 fusion.58
  387.6 4.1 fusion.57
  391.7 1.7 fusion.56
  393.4 1.8 fusion.55
  395.2 1.7 fusion.54
  396.9 1.8 fusion.53
  398.6 1.7 fusion.52
  400.3 1.8 fusion.51
  402.1 14.1 %reduce-scatter.7.cloned.1.call-done = bf16[128,512]{1,0:T(8,128)(2,1)} async-done(((bf16[1024,512]{1,0:T(8,128)(2,1)}), bf16[128,512]{1,0:T(8,128)(2,1)}) %reduce-scatter.7.cloned.1.call-update) | async-done | bytes 131088
  416.2 1.0 copy.19
  418.1 85.2 %reduce-scatter.5.cloned.1.call-done = f32[128,512]{0,1:T(8,128)} async-done(((f32[2048,512]{0,1:T(8,128)}), f32[128,512]{0,1:T(8,128)}) %reduce-scatter.5.cloned.1.call-update) | async-done | bytes 262160 | tf_op jit(solution)/shard_map/reduce_scatter | solution.py:121
  503.3 1.8 copy.16
  (102 shorter events, 21.3 us)
Async XLA Ops:
  7.2 54.1 %all-gather.12.cloned.1.call-start = ((), (), s32[]{:S(2)}) async-start(), calls=%async_computation.5 | async-start | bytes 1179648 | tf_op jit(solution)/shard_map/all_gather | solution.py:111
  7.9 94.6 %all-gather.10.cloned.1.call-start = ((), (), s32[]{:S(2)}) async-start(), calls=%async_computation.4 | async-start | bytes 2228224 | tf_op jit(solution)/shard_map/all_gather | solution.py:107
  10.2 21.0 %all-to-all-start = ((bf16[2,128,128]{2,0,1:T(2,128)(2,1)}), bf16[2,128,128]{2,0,1:T(2,128)(2,1)S(1)}, u32[]{:S(2)}, u32[]{:S(2)}) async-start(bf16[2,128,128]{2,0,1:T(2,128)(2,1)} %fusion.107), calls=%async_computation | async-start | bytes 131072 | tf_op jit(solution)/shard_map/all_to_all | solution.py:97
  31.3 29.3 %all-to-all-start.1 = ((bf16[2,128,128]{2,0,1:T(2,128)(2,1)}), bf16[2,128,128]{2,0,1:T(2,128)(2,1)S(1)}, u32[]{:S(2)}, u32[]{:S(2)}) async-start(bf16[2,128,128]{2,0,1:T(2,128)(2,1)} %bitcast.189), calls=%async_computation.1 | async-start | bytes 131072 | tf_op jit(solution)/shard_map/all_to_all | solution.py:96
  35.3 114.3 %all-gather.14.cloned.1.call-start = ((), (), s32[]{:S(2)}) async-start(), calls=%async_computation.6 | async-start | bytes 1114112 | tf_op jit(solution)/shard_map/all_gather | solution.py:108
  60.5 0.6 copy-start.16
  61.2 134.8 %all-gather.16.cloned.1.call-start = ((), (), s32[]{:S(2)}) async-start(), calls=%async_computation.8 | async-start | bytes 1114112 | tf_op jit(solution)/shard_map/all_gather | solution.py:15
  61.3 47.0 %copy-start.15 = (bf16[1024,512]{1,0:T(8,128)(2,1)S(1)}, bf16[1024,512]{1,0:T(8,128)(2,1)}, u32[]{:S(2)}) copy-start(bf16[1024,512]{1,0:T(8,128)(2,1)} %all-gather.12.cloned.1.call-done) | copy-start | bytes 3145732
  102.5 5.8 %copy-start.14 = (bf16[2048,512]{1,0:T(8,128)(2,1)S(1)}, bf16[2048,512]{1,0:T(8,128)(2,1)}, u32[]{:S(2)}) copy-start(bf16[2048,512]{1,0:T(8,128)(2,1)} %all-gather.10.cloned.1.call-done) | copy-start | bytes 6291460
  137.3 104.5 %all-gather.20.cloned.1.call-start = ((), (), s32[]{:S(2)}) async-start(), calls=%async_computation.10 | async-start | bytes 1114112 | tf_op jit(solution)/shard_map/all_gather | solution.py:15
  182.7 105.6 %all-gather.18.cloned.1.call-start = ((), (), s32[]{:S(2)}) async-start(), calls=%async_computation.9 | async-start | bytes 1114112 | tf_op jit(solution)/shard_map/all_gather | solution.py:15
  183.5 232.7 %reduce-scatter.7.cloned.1.call-start = ((), (), s32[]{:S(2)}) async-start(), calls=%async_computation.11 | async-start | bytes 1179648
  337.2 26.9 %copy-start.5 = (bf16[2048,1024]{0,1:T(8,128)(2,1)}, bf16[2048,1024]{0,1:T(8,128)(2,1)S(1)}, u32[]{:S(2)}) copy-start(bf16[2048,1024]{0,1:T(8,128)(2,1)S(1)} %get-tuple-element.236) | copy-start | bytes 12582916
  337.3 28.9 %copy-start.4 = (bf16[2048,1024]{0,1:T(8,128)(2,1)}, bf16[2048,1024]{0,1:T(8,128)(2,1)S(1)}, u32[]{:S(2)}) copy-start(bf16[2048,1024]{0,1:T(8,128)(2,1)S(1)} %get-tuple-element.237) | copy-start | bytes 12582916
  337.3 31.0 %copy-start.2 = (bf16[2048,1024]{0,1:T(8,128)(2,1)}, bf16[2048,1024]{0,1:T(8,128)(2,1)S(1)}, u32[]{:S(2)}) copy-start(bf16[2048,1024]{0,1:T(8,128)(2,1)S(1)} %get-tuple-element.238) | copy-start | bytes 12582916
  337.3 41.4 %copy-start = (bf16[2048,1024]{0,1:T(8,128)(2,1)}, bf16[2048,1024]{0,1:T(8,128)(2,1)S(1)}, u32[]{:S(2)}) copy-start(bf16[2048,1024]{0,1:T(8,128)(2,1)S(1)} %get-tuple-element.235) | copy-start | bytes 12582916
  364.1 12.6 %copy-start.6 = (bf16[2048,1024]{0,1:T(8,128)(2,1)}, bf16[2048,1024]{0,1:T(8,128)(2,1)S(1)}, u32[]{:S(2)}) copy-start(bf16[2048,1024]{0,1:T(8,128)(2,1)S(1)} %get-tuple-element.239) | copy-start | bytes 12582916
  364.1 6.2 %copy-start.12 = (bf16[2048,1024]{0,1:T(8,128)(2,1)S(1)}, bf16[2048,1024]{0,1:T(8,128)(2,1)}, u32[]{:S(2)}) copy-start(bf16[2048,1024]{0,1:T(8,128)(2,1)} %get-tuple-element.240) | copy-start | bytes 12582916
  366.2 6.3 %copy-start.10 = (bf16[2048,1024]{0,1:T(8,128)(2,1)S(1)}, bf16[2048,1024]{0,1:T(8,128)(2,1)}, u32[]{:S(2)}) copy-start(bf16[2048,1024]{0,1:T(8,128)(2,1)} %get-tuple-element.241) | copy-start | bytes 12582916
  368.3 6.3 %copy-start.8 = (bf16[2048,1024]{0,1:T(8,128)(2,1)S(1)}, bf16[2048,1024]{0,1:T(8,128)(2,1)}, u32[]{:S(2)}) copy-start(bf16[2048,1024]{0,1:T(8,128)(2,1)} %get-tuple-element.242) | copy-start | bytes 12582916
  383.2 120.1 %reduce-scatter.5.cloned.1.call-start = ((), (), s32[]{:S(2)}) async-start(), calls=%async_computation.7 | async-start | bytes 4456448 | tf_op jit(solution)/shard_map/reduce_scatter | solution.py:121
  383.5 8.2 %copy-start.3 = (bf16[2048,1024]{0,1:T(8,128)(2,1)S(1)}, bf16[2048,1024]{0,1:T(8,128)(2,1)}, u32[]{:S(2)}) copy-start(bf16[2048,1024]{0,1:T(8,128)(2,1)} %copy-done.2) | copy-start | bytes 12582916
  383.5 9.9 %copy-start.13 = (bf16[2048,1024]{0,1:T(8,128)(2,1)S(1)}, bf16[2048,1024]{0,1:T(8,128)(2,1)}, u32[]{:S(2)}) copy-start(bf16[2048,1024]{0,1:T(8,128)(2,1)} %get-tuple-element.240) | copy-start | bytes 12582916
  387.6 7.6 %copy-start.11 = (bf16[2048,1024]{0,1:T(8,128)(2,1)S(1)}, bf16[2048,1024]{0,1:T(8,128)(2,1)}, u32[]{:S(2)}) copy-start(bf16[2048,1024]{0,1:T(8,128)(2,1)} %get-tuple-element.241) | copy-start | bytes 12582916
  391.7 5.2 %copy-start.9 = (bf16[2048,1024]{0,1:T(8,128)(2,1)S(1)}, bf16[2048,1024]{0,1:T(8,128)(2,1)}, u32[]{:S(2)}) copy-start(bf16[2048,1024]{0,1:T(8,128)(2,1)} %get-tuple-element.242) | copy-start | bytes 12582916
  393.4 5.3 %copy-start.7 = (bf16[2048,1024]{0,1:T(8,128)(2,1)S(1)}, bf16[2048,1024]{0,1:T(8,128)(2,1)}, u32[]{:S(2)}) copy-start(bf16[2048,1024]{0,1:T(8,128)(2,1)} %copy-done.6) | copy-start | bytes 12582916
  395.2 5.2 %copy-start.1 = (bf16[2048,1024]{0,1:T(8,128)(2,1)S(1)}, bf16[2048,1024]{0,1:T(8,128)(2,1)}, u32[]{:S(2)}) copy-start(bf16[2048,1024]{0,1:T(8,128)(2,1)} %copy-done) | copy-start | bytes 12582916
Sparse Core Ops, SparseCore 0:
  9.6 37.7 all-gather.11
  49.8 52.7 all-gather.9
  105.4 44.1 all-gather.13
  152.4 43.5 all-gather.15
  198.2 43.5 all-gather.19
  244.7 43.5 all-gather.17
  383.3 32.8 reduce-scatter.6
  420.3 82.9 reduce-scatter.4
where the time goes:
time: 515 us; the launch traced here: 512 us
  waiting for transfers between devices  265 us (51%)
  matrix products  102 us (20%)
  other arithmetic  75.4 us (15%)
  blocking collectives  25.2 us (5%)
  starting transfers between devices  16.3 us (3%)
  between operations  14.3 us (3%)
  local copies, waits for them, and re-layouts  13.3 us (3%)
    all_gather x3, waiting for transfers between devices, combined_all(): gathered = jax.tree.map(lambda a: lax.all_gather(a, axis), part)  103 us
    reduce_scatter x1, waiting for transfers between devices, local(): lax.psum_scatter(q_total, 'col', scatter_dimension=0, tiled=True)  85.2 us
    convert_element_type x2, other arithmetic, grad_terms(): (weights / total * (expected_all[head][:, None] / total - counts) / HEADS...  43.5 us
    all_gather x1, waiting for transfers between devices, local(): lax.all_gather(queries, 'col', axis=0, tiled=True)  41.2 us
    dot_general x8, matrix products, head_scores(): lax.dot_general(q_part, k_part, (((1,), (1,)), ((), ())), preferred_eleme...  34 us
    dot_general x1, matrix products, local(): lax.dot_general(src_fwd, tgt_bwd, (((0,), (0,)), ((), ())), preferred_ele...  32.4 us
    all_gather x1, blocking collectives, local(): lax.all_gather(own_bwd, 'row', axis=1, tiled=True)  25.2 us
    dot_general x8, matrix products, grad_terms(): jnp.dot(grad, k_part, preferred_element_type=jnp.float32) * scale  18.5 us
  transfers between devices with their start and end apart: 10, of which 8 were waited for; matrix products, arithmetic and copies ran while one was open for 18% of the time, Pallas kernels for 0%

commit v1 on v0

v1 whole, which is shorter than its diff:
```python
import jax
import jax.numpy as jnp
from jax import lax
from jax.experimental import pallas as pl
from jax.experimental.pallas import tpu as pltpu
from jax.sharding import PartitionSpec as P

HEADS = 8
HEAD = 64
GRAIN = 32
SCALE = HEAD**-0.5
LOG_HEADS = 2.0794415416798357
NEG = -1e30
UB = 256
VC = 256
MESH = pl.DeviceIdType.MESH
VM = pl.BlockSpec(memory_space=pltpu.VMEM)
SM = pl.BlockSpec(memory_space=pltpu.SMEM)


def nn(a, b):
    return lax.dot_general(a, b, (((1,), (0,)), ((), ())), preferred_element_type=jnp.float32)


def nt(a, b):
    return lax.dot_general(a, b, (((1,), (1,)), ((), ())), preferred_element_type=jnp.float32)


def remote(src, dst, send, recv, peer):
    return pltpu.make_async_remote_copy(
        src_ref=src, dst_ref=dst, send_sem=send, recv_sem=recv, device_id=peer, device_id_type=MESH
    )


def enter(peers):
    barrier = pltpu.get_barrier_semaphore()
    for peer in peers:
        pl.semaphore_signal(barrier, inc=1, device_id=peer, device_id_type=MESH)
    pl.semaphore_wait(barrier, len(peers))


class Sends:
    def __init__(self, sems):
        self.sems = sems
        self.started = []

    def start(self, src, dst, recv, peer):
        copy = remote(src, dst, self.sems.at[len(self.started)], recv, peer)
        copy.start()
        self.started.append(copy)

    def drain(self):
        for copy in self.started:
            copy.wait_send()


def gather_kernel(q, k, sf, sb, qa, ka, fa, ba, send, recv_q, recv_f, recv_k, recv_b, in_f, in_b, own):
    row, col = lax.axis_index("row"), lax.axis_index("col")
    x, yh, core = col // 4, (col // 2) % 2, col % 2
    yl, z = row // 4, row % 4

    def at(r=None, c=None):
        return {"row": row if r is None else r, "col": col if c is None else c}

    def cslot(xx, yy, cc):
        return xx * 4 + yy * 2 + cc

    enter(
        [at(r=(row + d) % 8) for d in range(1, 8)] + [at(c=(col + d) % 16) for d in range(1, 16)]
    )
    sends = Sends(send)
    local = [
        pltpu.make_async_copy(q, qa.at[col], own.at[0]),
        pltpu.make_async_copy(k, ka.at[row], own.at[1]),
        pltpu.make_async_copy(sf.at[row], fa.at[:, col, row], own.at[2]),
        pltpu.make_async_copy(sb.at[:, col], ba.at[:, col, row], own.at[3]),
    ]
    for copy in local:
        copy.start()
    for d in range(1, 8):
        to = (row + d) % 8
        sends.start(sf.at[to], fa.at[:, col, row], in_f.at[row], at(r=to))
    for d in range(1, 16):
        to = (col + d) % 16
        sends.start(sb.at[:, to], ba.at[:, col, row], in_b.at[col], at(c=to))

    def q_part(slot, half=None):
        return qa.at[slot] if half is None else qa.at[slot, pl.ds(half * 64, 64)]

    def f_part(slot, half=None):
        return fa.at[:, slot] if half is None else fa.at[pl.ds(half * 8, 8), slot]

    def k_part(slot, half=None):
        return ka.at[slot] if half is None else ka.at[slot, pl.ds(half * 64, 64)]

    def b_part(slot, half=None):
        return ba.at[:, :, slot] if half is None else ba.at[pl.ds(half * 4, 4), :, slot]

    def src_slot(dx, dy, cc=None):
        return cslot((x + dx) % 4, (yh + dy) % 2, core if cc is None else cc)

    def tgt_slot(dz, dy):
        return ((yl + dy) % 2) * 4 + (z + dz) % 4

    def src_dev(dx, dy, dc=0):
        return at(c=cslot((x + dx) % 4, (yh + dy) % 2, (core + dc) % 2))

    def tgt_dev(dz, dy):
        return at(r=tgt_slot(dz, dy))

    source = (src_slot, src_dev, True)
    target = (tgt_slot, tgt_dev, False)
    streams = {
        "q": (q_part, recv_q, source),
        "f": (f_part, recv_f, source),
        "k": (k_part, recv_k, target),
        "b": (b_part, recv_b, target),
    }

    def push(kind, slot, peer, half=None):
        part, recv, _ = streams[kind]
        ref = part(slot, half)
        sends.start(ref, ref, recv.at[slot, 0 if half is None else half], peer)

    def arrived(kind, slot, half=None):
        part, recv, _ = streams[kind]
        ref = part(slot, half)
        remote(ref, ref, send.at[0], recv.at[slot, 0 if half is None else half], at()).wait_recv()

    def first(kind):
        slot_of, dev_of, pair = streams[kind][2]
        mine = slot_of(0, 0)
        push(kind, mine, dev_of(0, 1))
        push(kind, mine, dev_of(1, 0))
        push(kind, mine, dev_of(3, 0))
        if pair:
            push(kind, mine, dev_of(0, 0, 1))

    def second(kind):
        slot_of, dev_of, pair = streams[kind][2]
        other = slot_of(0, 1)
        arrived(kind, other)
        push(kind, other, dev_of(1, 0))
        push(kind, other, dev_of(3, 0))
        if pair:
            push(kind, other, dev_of(0, 0, 1))

    def relay(kind, dy):
        slot_of, dev_of, pair = streams[kind][2]
        for step, half in ((3, 0), (1, 1)):
            slot = slot_of(step, dy)
            arrived(kind, slot)
            push(kind, slot, dev_of(4 - step, 0), half)
            if pair:
                push(kind, slot, dev_of(0, 0, 1))

    def last(kind, dy):
        slot_of, dev_of, pair = streams[kind][2]
        slot = slot_of(2, dy)
        arrived(kind, slot, 0)
        arrived(kind, slot, 1)
        if pair:
            push(kind, slot, dev_of(0, 0, 1))

    local[0].wait()
    local[1].wait()
    first("q")
    first("k")
    local[2].wait()
    for d in range(1, 8):
        frm = (row + d) % 8
        ref = fa.at[:, col, frm]
        remote(ref, ref, send.at[0], in_f.at[frm], at()).wait_recv()
    first("f")
    local[3].wait()
    for d in range(1, 16):
        frm = (col + d) % 16
        ref = ba.at[:, frm, row]
        remote(ref, ref, send.at[0], in_b.at[frm], at()).wait_recv()
    first("b")
    second("k")
    second("q")
    relay("k", 0)
    relay("q", 0)
    second("b")
    second("f")
    relay("k", 1)
    relay("q", 1)
    relay("b", 0)
    relay("f", 0)
    relay("b", 1)
    relay("f", 1)
    for kind in ("k", "q", "b", "f"):
        last(kind, 0)
        last(kind, 1)
    for kind in ("q", "f"):
        for dx in range(4):
            for dy in range(2):
                arrived(kind, src_slot(dx, dy, 1 - core))
    sends.drain()


def gather(q, k, sf, sb):
    bf = jnp.bfloat16
    return pl.pallas_call(
        gather_kernel,
        in_specs=[VM] * 4,
        out_specs=[VM] * 4,
        out_shape=[
            jax.ShapeDtypeStruct((16, 128, 512), bf),
            jax.ShapeDtypeStruct((8, 128, 512), bf),
            jax.ShapeDtypeStruct((16, 16, 8, 2, 128), bf),
            jax.ShapeDtypeStruct((8, 16, 8, 2, 128), bf),
        ],
        scratch_shapes=[
            pltpu.SemaphoreType.DMA((100,)),
            pltpu.SemaphoreType.DMA((16, 2)),
            pltpu.SemaphoreType.DMA((16, 2)),
            pltpu.SemaphoreType.DMA((8, 2)),
            pltpu.SemaphoreType.DMA((8, 2)),
            pltpu.SemaphoreType.DMA((8,)),
            pltpu.SemaphoreType.DMA((16,)),
            pltpu.SemaphoreType.DMA((4,)),
        ],
        compiler_params=pltpu.CompilerParams(
            collective_id=0, has_side_effects=True, vmem_limit_bytes=40 << 20
        ),
        name="gather",
    )(q, k, sf, sb)


def merge_kernel(part, out, landed, mine, send, recv, recv2, own):
    row, col = lax.axis_index("row"), lax.axis_index("col")
    peers = [{"row": row, "col": (col + d) % 16} for d in range(1, 16)]
    enter(peers)
    sends = Sends(send)
    keep = pltpu.make_async_copy(part.at[col], landed.at[col], own.at[0])
    keep.start()
    for d, peer in enumerate(peers):
        sends.start(part.at[peer["col"]], landed.at[col], recv.at[col], peer)
    keep.wait()
    for peer in peers:
        ref = landed.at[peer["col"]]
        remote(ref, ref, send.at[0], recv.at[peer["col"]], peer).wait_recv()
    logs = landed[:, 0:8]
    top = jnp.max(logs, axis=0)
    weight = jnp.exp(logs - top[None])
    total = jnp.sum(weight, axis=0)
    mean = jnp.sum(weight * landed[:, 8:16], axis=0) / total
    mine[0:8, :] = top + jnp.log(total) + LOG_HEADS
    mine[8:16, :] = mean
    keep = pltpu.make_async_copy(mine, out.at[col], own.at[1])
    keep.start()
    for peer in peers:
        sends.start(mine, out.at[col], recv2.at[col], peer)
    keep.wait()
    for peer in peers:
        ref = out.at[peer["col"]]
        remote(ref, ref, send.at[0], recv2.at[peer["col"]], peer).wait_recv()
    sends.drain()


def merge(part):
    return pl.pallas_call(
        merge_kernel,
        in_specs=[VM],
        out_specs=VM,
        out_shape=jax.ShapeDtypeStruct((16, 16, 128), jnp.float32),
        scratch_shapes=[
            pltpu.VMEM((16, 16, 128), jnp.float32),
            pltpu.VMEM((16, 128), jnp.float32),
            pltpu.SemaphoreType.DMA((30,)),
            pltpu.SemaphoreType.DMA((16,)),
            pltpu.SemaphoreType.DMA((16,)),
            pltpu.SemaphoreType.DMA((2,)),
        ],
        compiler_params=pltpu.CompilerParams(collective_id=1, has_side_effects=True),
        name="merge",
    )(part)


def reduce_kernel(qp, kp, qo, ko, pair_in, pair_sum, ring_q, ring_k, out_q, out_k, last_q, last_k, send, recv):
    row, col = lax.axis_index("row"), lax.axis_index("col")
    x, yh, core = col // 4, (col // 2) % 2, col % 2
    yl, z = row // 4, row % 4

    def q_dev(xx, yy, cc):
        return {"row": row, "col": xx * 4 + yy * 2 + cc}

    def k_dev(yy, zz):
        return {"row": yy * 4 + zz, "col": col}

    sibling = q_dev(x, yh, 1 - core)
    ring_x = [(x + d) % 4 for d in range(1, 4)]
    ring_z = [(z + d) % 4 for d in range(1, 4)]
    enter(
        [sibling, q_dev(x, 1 - yh, core), k_dev(1 - yl, z)]
        + [q_dev(xx, yh, core) for xx in ring_x]
        + [k_dev(yl, zz) for zz in ring_z]
    )
    sends = Sends(send)
    for xx in ring_x + [x]:
        sends.start(
            qp.at[xx, :, 1 - core], pair_in.at[xx], recv.at[0, xx], sibling
        )
    for zz in ring_z:
        sends.start(kp.at[:, zz], ring_k.at[z], recv.at[1, z], k_dev(yl, zz))
    for xx in ring_x + [x]:
        ref = pair_in.at[xx]
        remote(ref, ref, send.at[0], recv.at[0, xx], sibling).wait_recv()
        pair_sum[xx] = (
            qp[xx, :, core].astype(jnp.float32) + pair_in[xx].astype(jnp.float32)
        ).astype(jnp.bfloat16)
    for xx in ring_x:
        sends.start(pair_sum.at[xx], ring_q.at[x], recv.at[2, x], q_dev(xx, yh, core))

    def ring_total(own, landed, row_of, ring, which, peer):
        for at in ring:
            ref = landed.at[at]
            remote(ref, ref, send.at[0], recv.at[which, at], peer).wait_recv()
        totals = []
        for half in range(2):
            total = own(half).astype(jnp.float32)
            for at in ring:
                total = total + landed[at, half].astype(jnp.float32)
            totals.append(total)
        return totals

    def finish(own, landed, ring, which, pos, stage, last, out, peer, slot):
        for at in ring:
            ref = landed.at[at]
            remote(ref, ref, send.at[0], recv.at[which, at], peer).wait_recv()
        total = own(1 - pos).astype(jnp.float32)
        for at in ring:
            total = total + landed[at, 1 - pos].astype(jnp.float32)
        stage[...] = total.astype(jnp.bfloat16)
        sends.start(stage, last, recv.at[3, slot], peer)
        total = own(pos).astype(jnp.float32)
        for at in ring:
            total = total + landed[at, pos].astype(jnp.float32)
        out[...] = total

    pair_y = q_dev(x, 1 - yh, core)
    pair_r = k_dev(1 - yl, z)
    finish(lambda y: kp[y, z], ring_k, ring_z, 1, yl, out_k, last_k, ko, pair_r, 0)
    finish(lambda y: pair_sum[x, y], ring_q, ring_x, 2, yh, out_q, last_q, qo, pair_y, 1)
    remote(last_k, last_k, send.at[0], recv.at[3, 0], pair_r).wait_recv()
    ko[...] += last_k[...].astype(jnp.float32)
    remote(last_q, last_q, send.at[0], recv.at[3, 1], pair_y).wait_recv()
    qo[...] += last_q[...].astype(jnp.float32)
    sends.drain()


def reduce(qp, kp):
    bf = jnp.bfloat16
    return pl.pallas_call(
        reduce_kernel,
        in_specs=[VM] * 2,
        out_specs=[VM] * 2,
        out_shape=[jax.ShapeDtypeStruct((128, 512), jnp.float32)] * 2,
        scratch_shapes=[
            pltpu.VMEM((4, 2, 128, 512), bf),
            pltpu.VMEM((4, 2, 128, 512), bf),
            pltpu.VMEM((4, 2, 128, 512), bf),
            pltpu.VMEM((4, 2, 128, 512), bf),
            pltpu.VMEM((128, 512), bf),
            pltpu.VMEM((128, 512), bf),
            pltpu.VMEM((128, 512), bf),
            pltpu.VMEM((128, 512), bf),
            pltpu.SemaphoreType.DMA((16,)),
            pltpu.SemaphoreType.DMA((4, 4)),
        ],
        compiler_params=pltpu.CompilerParams(
            collective_id=2, has_side_effects=True, vmem_limit_bytes=40 << 20
        ),
        name="reduce",
    )(qp, kp)


def mask_keys(k_ref, km):
    half = lax.broadcasted_iota(jnp.int32, (128, 128), 1) < HEAD
    for block in range(8):
        for h in range(HEADS):
            kk = k_ref[block, :, (h // 2) * 128 : (h // 2 + 1) * 128]
            keep = half if h % 2 == 0 else jnp.logical_not(half)
            km[h, block * 128 : (block + 1) * 128, :] = jnp.where(keep, kk, jnp.zeros_like(kk))


def tile_terms(i, j, q_ref, f_ref, bt, grains, pu_ref):
    f = jnp.concatenate([f_ref[2 * i], f_ref[2 * i + 1]], axis=1)
    counts = nn(bt[pl.ds(pl.multiple_of(j * VC, VC), VC), :], f)
    off = lax.broadcasted_iota(jnp.int32, (GRAIN, UB), 0)
    per = VC // GRAIN
    pv = jnp.concatenate([off + GRAIN * grains[j * per + t] for t in range(per)], axis=0)
    valid = pv >= pu_ref[pl.ds(i, 1), :]
    return counts, valid


def queries_of(i, q_ref):
    q = jnp.concatenate([q_ref[2 * i], q_ref[2 * i + 1]], axis=0)
    return q * jnp.bfloat16(SCALE)


def stats_kernel(q_ref, k_ref, f_ref, b_ref, grains, pu_ref, out, km, bt):
    mask_keys(k_ref, km)
    for block in range(8):
        bt[block * 128 : (block + 1) * 128, :] = b_ref[block].T

    def sources(i, _):
        q = queries_of(i, q_ref)

        def targets(j, state):
            counts, valid = tile_terms(i, j, q_ref, f_ref, bt, grains, pu_ref)
            vs = pl.multiple_of(j * VC, VC)
            after = []
            for h in range(HEADS):
                top, total, expect = state[h]
                s = nt(km[h, pl.ds(vs, VC), :], q[:, (h // 2) * 128 : (h // 2 + 1) * 128])
                s = jnp.where(valid, s, NEG)
                higher = jnp.maximum(top, jnp.max(s, axis=0, keepdims=True))
                w = jnp.exp(s - higher)
                w = jnp.where(valid, w, 0.0)
                shrink = jnp.exp(top - higher)
                total = total * shrink + jnp.sum(w, axis=0, keepdims=True)
                expect = expect * shrink + jnp.sum(w * counts, axis=0, keepdims=True)
                after.append((higher, total, expect))
            return tuple(after)

        zero = jnp.zeros((1, UB), jnp.float32)
        state = lax.fori_loop(
            0, 1024 // VC, targets, tuple((zero + NEG, zero, zero) for _ in range(HEADS))
        )
        for h in range(HEADS):
            top, total, expect = state[h]
            some = total > 0.0
            safe = jnp.where(some, total, 1.0)
            log = jnp.where(some, top + jnp.log(safe), NEG)
            mean = expect / safe
            for t in range(UB // 128):
                out[2 * i + t, h : h + 1, :] = log[:, t * 128 : (t + 1) * 128]
                out[2 * i + t, HEADS + h : HEADS + h + 1, :] = mean[:, t * 128 : (t + 1) * 128]
        return 0

    lax.fori_loop(0, 2048 // UB, sources, 0)


def stats(q, k, f, b, grains, pu):
    return pl.pallas_call(
        stats_kernel,
        in_specs=[VM] * 4 + [SM, VM],
        out_specs=VM,
        out_shape=jax.ShapeDtypeStruct((16, 16, 128), jnp.float32),
        scratch_shapes=[
            pltpu.VMEM((HEADS, 1024, 128), jnp.bfloat16),
            pltpu.VMEM((1024, 256), jnp.bfloat16),
        ],
        compiler_params=pltpu.CompilerParams(vmem_limit_bytes=40 << 20),
        name="stats",
    )(q, k, f, b, grains, pu)


def grads_kernel(q_ref, k_ref, f_ref, b_ref, grains, pu_ref, st, qg, kg, km, kt, bt, qacc, kacc):
    mask_keys(k_ref, km)
    for block in range(8):
        bt[block * 128 : (block + 1) * 128, :] = b_ref[block].T
        kt[:, block * 128 : (block + 1) * 128] = k_ref[block].T
    kacc[...] = jnp.zeros_like(kacc)
    low = lax.broadcasted_iota(jnp.int32, (VC, 128), 1) < HEAD

    def sources(i, _):
        q = queries_of(i, q_ref)
        both = jnp.concatenate([st[2 * i], st[2 * i + 1]], axis=1)
        qacc[...] = jnp.zeros_like(qacc)

        def targets(j, _):
            counts, valid = tile_terms(i, j, q_ref, f_ref, bt, grains, pu_ref)
            vs = pl.multiple_of(j * VC, VC)
            pair = []
            for h in range(HEADS):
                qp = q[:, (h // 2) * 128 : (h // 2 + 1) * 128]
                s = nt(km[h, pl.ds(vs, VC), :], qp)
                w = jnp.exp(jnp.where(valid, s - both[h : h + 1], NEG))
                g = (w * (both[HEADS + h : HEADS + h + 1] - counts)).astype(jnp.bfloat16)
                hs = slice(h * HEAD, (h + 1) * HEAD)
                qacc[hs, :] += nn(kt[hs, pl.ds(vs, VC)], g)
                pair.append(nn(g, qp))
                if h % 2:
                    cols = slice((h // 2) * 128, (h // 2 + 1) * 128)
                    kacc[pl.ds(vs, VC), cols] += jnp.where(low, pair[-2], pair[-1])
            return 0

        lax.fori_loop(0, 1024 // VC, targets, 0)
        turned = (qacc[...] * SCALE).T.astype(jnp.bfloat16)
        for t in range(UB // 128):
            qg[2 * i + t] = turned[t * 128 : (t + 1) * 128]
        return 0

    lax.fori_loop(0, 2048 // UB, sources, 0)
    for block in range(8):
        kg[block] = kacc[block * 128 : (block + 1) * 128, :].astype(jnp.bfloat16)


def grads(q, k, f, b, grains, pu, st):
    bf = jnp.bfloat16
    return pl.pallas_call(
        grads_kernel,
        in_specs=[VM] * 4 + [SM, VM, VM],
        out_specs=[VM] * 2,
        out_shape=[
            jax.ShapeDtypeStruct((16, 128, 512), bf),
            jax.ShapeDtypeStruct((8, 128, 512), bf),
        ],
        scratch_shapes=[
            pltpu.VMEM((HEADS, 1024, 128), bf),
            pltpu.VMEM((512, 1024), bf),
            pltpu.VMEM((1024, 256), bf),
            pltpu.VMEM((512, UB), jnp.float32),
            pltpu.VMEM((1024, 512), jnp.float32),
        ],
        compiler_params=pltpu.CompilerParams(vmem_limit_bytes=40 << 20),
        name="grads",
    )(q, k, f, b, grains, pu, st)


def local(queries, keys, fwd_table, bwd_table, step_weight, block_order):
    row_id = lax.axis_index("row")
    col_id = lax.axis_index("col")
    scaled = (bwd_table.astype(jnp.float32) * step_weight[:, None]).astype(jnp.bfloat16)
    sf = fwd_table.reshape(2, 8, 16, 128).transpose(1, 2, 0, 3)
    sb = scaled.reshape(2, 8, 16, 128).transpose(1, 2, 0, 3)
    grid = block_order.reshape(8, 16, 4)
    line = lax.dynamic_index_in_dim(grid, row_id, 0, keepdims=False).reshape(64)
    column = lax.dynamic_index_in_dim(grid, col_id, 1, keepdims=False).reshape(32)
    offsets = jnp.arange(GRAIN, dtype=jnp.int32)
    pu = (line[:, None] * GRAIN + offsets[None, :]).reshape(2048 // UB, UB)
    q, k, f, b = gather(queries, keys, sf, sb)
    f = f.reshape(16, 256, 128)
    b = b.reshape(8, 256, 128)
    merged = merge(stats(q, k, f, b, column, pu))
    qg, kg = grads(q, k, f, b, column, pu, merged)
    return reduce(qg.reshape(4, 2, 2, 128, 512), kg.reshape(2, 4, 128, 512))


def solution(mesh):
    return jax.shard_map(
        local,
        mesh=mesh,
        in_specs=(
            P(("row", "col"), None),
            P(("row", "col"), None),
            P(("row", "col"), None),
            P(("row", "col"), None),
            P(("row", "col")),
            P(),
        ),
        out_specs=(P(("row", "col"), None), P(("row", "col"), None)),
        check_vma=False,
    )
```

time: 515 us -> 184 us (0.36)
  waiting for transfers between devices: 265 us -> 0 us
  Pallas kernels: 0 us -> 171 us
  matrix products: 102 us -> 0 us
  other arithmetic: 75.4 us -> 0.98 us
  blocking collectives: 25.2 us -> 0 us
  starting transfers between devices: 16.3 us -> 0 us
  between operations: 14.3 us -> 0.74 us
    pallas_call x0 -> x5, Pallas kernels: none -> 171 us  [the longest x1 59.2 us: grads(): pl.pallas_call(grads_kernel, in_specs=[VM] * 4 + [SM, VM, VM], out_specs=...]
    all_gather x6 -> x0, waiting for transfers between devices: 156 us -> none  [the longest x3 103 us: combined_all(): gathered = jax.tree.map(lambda a: lax.all_gather(a, axis), part)]
    dot_general x25 -> x0, matrix products: 102 us -> none  [the longest x8 34 us: head_scores(): lax.dot_general(q_part, k_part, (((1,), (1,)), ((), ())), preferred_eleme...]
    reduce_scatter x1 -> x0, waiting for transfers between devices: 85.2 us -> none  [local(): lax.psum_scatter(q_total, 'col', scatter_dimension=0, tiled=True)]
    convert_element_type x2 -> x1, other arithmetic: 43.5 us -> 0.96 us  [local(): (bwd_table.astype(jnp.float32) * step_weight[:, None]).astype(jnp.bfloat16)]
    add x32 -> x1, other arithmetic: 27.8 us -> 0.01 us  [local(): pu = (line[:, None] * GRAIN + offsets[None, :]).reshape(2048 // UB, UB)]
    all_gather x1 -> x0, blocking collectives: 25.2 us -> none  [local(): lax.all_gather(own_bwd, 'row', axis=1, tiled=True)]
    unnamed x9 -> x0, waiting for transfers between devices: 15.6 us -> none
  transfers between devices with their start and end apart: 10 -> 0, of which waited for: 8 -> 0; matrix products, arithmetic and copies ran while one was open for 18% -> 0% of each run, Pallas kernels for 0% -> 0%
where the time goes in v1:
time: 184 us
  Pallas kernels  171 us (93%)
  local copies, waits for them, and re-layouts  10.8 us (6%)
    pallas_call x1, Pallas kernels, grads(): pl.pallas_call(grads_kernel, in_specs=[VM] * 4 + [SM, VM, VM], out_specs=...  59.2 us
    pallas_call x1, Pallas kernels, stats(): pl.pallas_call(stats_kernel, in_specs=[VM] * 4 + [SM, VM], out_specs=VM,...  38.8 us
    pallas_call x1, Pallas kernels, gather(): pl.pallas_call(gather_kernel, in_specs=[VM] * 4, out_specs=[VM] * 4, out_...  33.6 us
    pallas_call x1, Pallas kernels, reduce(): pl.pallas_call(reduce_kernel, in_specs=[VM] * 2, out_specs=[VM] * 2, out_...  23.8 us
    pallas_call x1, Pallas kernels, merge(): pl.pallas_call(merge_kernel, in_specs=[VM], out_specs=VM, out_shape=jax.S...  15.7 us
    unnamed x20, local copies, waits for them, and re-layouts  9.64 us

profile of v1, /device:TPU:1, one launch (start us, length us, event | category | flops | bytes accessed | tf_op | source)
XLA Modules:
  0.0 183.7 jit_solution(3738294274366866546)
XLA Ops:
  0.6 0.1 add.33
  0.7 0.8 reshape.49
  1.6 0.1 mul.26
  1.6 0.1 reshape.50.grains
  1.7 0.1 add.30
  1.8 0.1 add.31
  1.9 1.0 multiply_convert_fusion
  2.8 0.0 copy-start.6
  2.9 0.9 copy-done.6
  3.7 0.0 copy-start.7
  3.7 0.9 copy-done.7
  4.7 0.0 copy-start.8
  4.7 0.8 copy-done.8
  5.5 33.6 %gather.1 = (bf16[16,128,512]{2,1,0:T(8,128)(2,1)S(1)}, bf16[8,128,512]{2,1,0:T(8,128)(2,1)S(1)}, bf16[16,16,8,2,128]{4,3,2,1,0:T(2,128)(2,1)S(1)}, bf16[8,16,8,2,128]{4,3,2,1,0:T(2,128)(2,1)S(1)}) custom-call(bf16[128,512]{1,0:T(8,128)(2,1)S(1)} %copy-done.6, bf16[128,512]{1,0:T(8,128)(2,1)S(1)} %copy-done.7, bf16[8,16,2,128]{3,2,1,0:T(2,128)(2,1)S(1)} %bitcast.17, ...), custom_call_target="tpu_custom_call" | custom-call | tf_op jit(solution)/shard_map/gather/pallas_call | solution.py:205
  39.1 38.8 %stats.1.part = f32[16,16,128]{2,1,0:T(8,128)S(1)} custom-call(bf16[16,128,512]{2,1,0:T(8,128)(2,1)S(1)} %get-tuple-element.8.q_ref, bf16[8,128,512]{2,1,0:T(8,128)(2,1)S(1)} %get-tuple-element.9.k_ref, bf16[16,256,128]{2,1,0:T(8,128)(2,1)S(1)} %bitcast.10, bf16[8,256,128]{2,1,0:T(8,128)(2,1)S(1)} %bitcast.12, s32[32]{0:T(128)S(1)} %reshape.50.grains, ...), custom_call_target="tpu_custom_call" | custom-call | tf_op jit(solution)/shard_map/stats/pallas_call | solution.py:448
  77.9 0.0 copy-start
  77.9 1.0 copy-done
  78.9 0.0 copy-start.2
  78.9 0.8 copy-done.2
  79.7 0.0 copy-start.5
  79.7 0.7 copy-done.5
  80.4 15.7 %merge.1.st = f32[16,16,128]{2,1,0:T(8,128)} custom-call(f32[16,16,128]{2,1,0:T(8,128)} %copy-done.5), custom_call_target="tpu_custom_call" | custom-call | tf_op jit(solution)/shard_map/merge/pallas_call | solution.py:264
  96.1 0.0 copy-start.1
  96.1 1.2 copy-done.1
  97.3 0.0 copy-start.3
  97.3 1.0 copy-done.3
  98.4 0.0 copy-start.4
  98.4 0.9 copy-done.4
  99.3 59.2 %grads.1 = (bf16[16,128,512]{2,1,0:T(8,128)(2,1)S(1)}, bf16[8,128,512]{2,1,0:T(8,128)(2,1)S(1)}) custom-call(bf16[16,128,512]{2,1,0:T(8,128)(2,1)S(1)} %get-tuple-element.8.q_ref, bf16[8,128,512]{2,1,0:T(8,128)(2,1)S(1)} %get-tuple-element.9.k_ref, bf16[16,256,128]{2,1,0:T(8,128)(2,1)S(1)} %bitcast.11, bf16[8,256,128]{2,1,0:T(8,128)(2,1)S(1)} %bitcast.13, ...), custom_call_target="tpu_custom_call" | custom-call | tf_op jit(solution)/shard_map/grads/pallas_call | solution.py:505
  158.5 23.8 %reduce.5 = (f32[128,512]{1,0:T(8,128)S(1)}, f32[128,512]{1,0:T(8,128)S(1)}) custom-call(bf16[4,2,2,128,512]{4,3,2,1,0:T(8,128)(2,1)S(1)} %bitcast.14, bf16[2,4,128,512]{3,2,1,0:T(8,128)(2,1)S(1)} %bitcast.15), custom_call_target="tpu_custom_call" | custom-call | tf_op jit(solution)/shard_map/reduce/pallas_call | solution.py:356
  182.3 0.7 copy.10
  183.0 0.7 copy.11
  (4 shorter events, 0.0 us)
Async XLA Ops:
  2.8 0.9 copy-start.6
  3.7 0.9 copy-start.7
  4.7 0.8 copy-start.8
  77.9 1.0 copy-start
  78.9 0.8 copy-start.2
  79.7 0.7 copy-start.5
  96.1 1.2 copy-start.1
  97.3 1.0 copy-start.3
  98.4 0.9 copy-start.4

commit v2 on v1

--- a/solution.py
+++ b/solution.py
@@ -11,8 +11,11 @@
 SCALE = HEAD**-0.5
 LOG_HEADS = 2.0794415416798357
 NEG = -1e30
-UB = 256
-VC = 256
+TOP = -1e29
+NU = 64
+NV = 32
+UB1, VC1 = 256, 128
+UB2, VC2 = 256, 128
 MESH = pl.DeviceIdType.MESH
 VM = pl.BlockSpec(memory_space=pltpu.VMEM)
 SM = pl.BlockSpec(memory_space=pltpu.SMEM)
@@ -223,7 +226,7 @@
             pltpu.SemaphoreType.DMA((4,)),
         ],
         compiler_params=pltpu.CompilerParams(
-            collective_id=0, has_side_effects=True, vmem_limit_bytes=40 << 20
+            collective_id=0, has_side_effects=True, vmem_limit_bytes=16 << 20
         ),
         name="gather",
     )(q, k, sf, sb)
@@ -274,7 +277,9 @@
             pltpu.SemaphoreType.DMA((16,)),
             pltpu.SemaphoreType.DMA((2,)),
         ],
-        compiler_params=pltpu.CompilerParams(collective_id=1, has_side_effects=True),
+        compiler_params=pltpu.CompilerParams(
+            collective_id=1, has_side_effects=True, vmem_limit_bytes=4 << 20
+        ),
         name="merge",
     )(part)
 
@@ -314,18 +319,6 @@
     for xx in ring_x:
         sends.start(pair_sum.at[xx], ring_q.at[x], recv.at[2, x], q_dev(xx, yh, core))
 
-    def ring_total(own, landed, row_of, ring, which, peer):
-        for at in ring:
-            ref = landed.at[at]
-            remote(ref, ref, send.at[0], recv.at[which, at], peer).wait_recv()
-        totals = []
-        for half in range(2):
-            total = own(half).astype(jnp.float32)
-            for at in ring:
-                total = total + landed[at, half].astype(jnp.float32)
-            totals.append(total)
-        return totals
-
     def finish(own, landed, ring, which, pos, stage, last, out, peer, slot):
         for at in ring:
             ref = landed.at[at]
@@ -371,155 +364,247 @@
             pltpu.SemaphoreType.DMA((4, 4)),
         ],
         compiler_params=pltpu.CompilerParams(
-            collective_id=2, has_side_effects=True, vmem_limit_bytes=40 << 20
+            collective_id=2, has_side_effects=True, vmem_limit_bytes=16 << 20
         ),
         name="reduce",
     )(qp, kp)
 
 
-def mask_keys(k_ref, km):
+def mask_keys(ks, km):
     half = lax.broadcasted_iota(jnp.int32, (128, 128), 1) < HEAD
     for block in range(8):
+        rows = slice(block * 128, (block + 1) * 128)
         for h in range(HEADS):
-            kk = k_ref[block, :, (h // 2) * 128 : (h // 2 + 1) * 128]
+            kk = ks[rows, (h // 2) * 128 : (h // 2 + 1) * 128]
             keep = half if h % 2 == 0 else jnp.logical_not(half)
-            km[h, block * 128 : (block + 1) * 128, :] = jnp.where(keep, kk, jnp.zeros_like(kk))
-
-
-def tile_terms(i, j, q_ref, f_ref, bt, grains, pu_ref):
-    f = jnp.concatenate([f_ref[2 * i], f_ref[2 * i + 1]], axis=1)
-    counts = nn(bt[pl.ds(pl.multiple_of(j * VC, VC), VC), :], f)
-    off = lax.broadcasted_iota(jnp.int32, (GRAIN, UB), 0)
-    per = VC // GRAIN
-    pv = jnp.concatenate([off + GRAIN * grains[j * per + t] for t in range(per)], axis=0)
-    valid = pv >= pu_ref[pl.ds(i, 1), :]
-    return counts, valid
-
-
-def queries_of(i, q_ref):
-    q = jnp.concatenate([q_ref[2 * i], q_ref[2 * i + 1]], axis=0)
-    return q * jnp.bfloat16(SCALE)
-
-
-def stats_kernel(q_ref, k_ref, f_ref, b_ref, grains, pu_ref, out, km, bt):
-    mask_keys(k_ref, km)
+            km[h, rows, :] = jnp.where(keep, kk, jnp.zeros_like(kk))
+
+
+def order_of(meta, which, g):
+    return meta[which * NU + g]
+
+
+def place_of(meta, which, g):
+    return meta[NU + NV + which * NU + g]
+
+
+def rows_of(g):
+    return pl.ds(pl.multiple_of(g * GRAIN, GRAIN), GRAIN)
+
+
+def chunk_bounds(meta, i, ub, vc):
+    low = place_of(meta, 0, i * (ub // GRAIN))
+    high = place_of(meta, 0, (i + 1) * (ub // GRAIN) - 1)
+    per = vc // GRAIN
+    first = jnp.int32(0)
+    full = jnp.int32(0)
+    for j in range(NV // per):
+        first += (place_of(meta, 1, (j + 1) * per - 1) < low).astype(jnp.int32)
+        full += (place_of(meta, 1, j * per) <= high).astype(jnp.int32)
+    return first, full
+
+
+def chunk_valid(meta, pu, j, ub, vc):
+    off = lax.broadcasted_iota(jnp.int32, (GRAIN, ub), 0)
+    per = vc // GRAIN
+    pv = jnp.concatenate(
+        [off + GRAIN * place_of(meta, 1, j * per + t) for t in range(per)], axis=0
+    )
+    return pv >= pu
+
+
+def stats_kernel(q_ref, k_ref, f_ref, b_ref, meta, pu_ref, out, qs, ks, fs, bs, km, ft, bt, run_m, run_t, run_e):
+    ub, vc = UB1, VC1
+    for block in range(16):
+        ft[block * 128 : (block + 1) * 128, :] = f_ref[block].T
     for block in range(8):
         bt[block * 128 : (block + 1) * 128, :] = b_ref[block].T
 
+    def sort_sources(g, _):
+        frm = rows_of(order_of(meta, 0, g))
+        qs[rows_of(g), :] = q_ref[frm, :] * jnp.bfloat16(SCALE)
+        fs[rows_of(g), :] = ft[frm, :]
+        return 0
+
+    def sort_targets(g, _):
+        frm = rows_of(order_of(meta, 1, g))
+        ks[rows_of(g), :] = k_ref[frm, :]
+        bs[rows_of(g), :] = bt[frm, :]
+        return 0
+
+    lax.fori_loop(0, NU, sort_sources, 0)
+    lax.fori_loop(0, NV, sort_targets, 0)
+    mask_keys(ks, km)
+
     def sources(i, _):
-        q = queries_of(i, q_ref)
-
-        def targets(j, state):
-            counts, valid = tile_terms(i, j, q_ref, f_ref, bt, grains, pu_ref)
-            vs = pl.multiple_of(j * VC, VC)
-            after = []
+        us = pl.ds(pl.multiple_of(i * ub, ub), ub)
+        first, full = chunk_bounds(meta, i, ub, vc)
+        run_m[...] = jnp.full_like(run_m, TOP)
+        run_t[...] = jnp.zeros_like(run_t)
+        run_e[...] = jnp.zeros_like(run_e)
+
+        def targets(j, masked):
+            vs = pl.ds(pl.multiple_of(j * vc, vc), vc)
+            counts = nt(bs[vs, :], fs[us, :]).reshape(vc // 8, 8, ub)
+            if masked:
+                valid = chunk_valid(meta, pu_ref[pl.ds(i, 1), :], j, ub, vc)
             for h in range(HEADS):
-                top, total, expect = state[h]
-                s = nt(km[h, pl.ds(vs, VC), :], q[:, (h // 2) * 128 : (h // 2 + 1) * 128])
-                s = jnp.where(valid, s, NEG)
-                higher = jnp.maximum(top, jnp.max(s, axis=0, keepdims=True))
-                w = jnp.exp(s - higher)
-                w = jnp.where(valid, w, 0.0)
-                shrink = jnp.exp(top - higher)
-                total = total * shrink + jnp.sum(w, axis=0, keepdims=True)
-                expect = expect * shrink + jnp.sum(w * counts, axis=0, keepdims=True)
-                after.append((higher, total, expect))
-            return tuple(after)
-
-        zero = jnp.zeros((1, UB), jnp.float32)
-        state = lax.fori_loop(
-            0, 1024 // VC, targets, tuple((zero + NEG, zero, zero) for _ in range(HEADS))
-        )
+                s = nt(km[h, vs, :], qs[us, (h // 2) * 128 : (h // 2 + 1) * 128])
+                if masked:
+                    s = jnp.where(valid, s, NEG)
+                s = s.reshape(vc // 8, 8, ub)
+                old = run_m[h]
+                new = jnp.maximum(old, jnp.max(s, axis=0))
+                w = jnp.exp(s - new[None])
+                shrink = jnp.exp(old - new)
+                run_m[h] = new
+                run_t[h] = run_t[h] * shrink + jnp.sum(w, axis=0)
+                run_e[h] = run_e[h] * shrink + jnp.sum(w * counts, axis=0)
+
+        def masked_step(j, _):
+            targets(j, True)
+            return 0
+
+        def open_step(j, _):
+            targets(j, False)
+            return 0
+
+        lax.fori_loop(first, full, masked_step, 0)
+        lax.fori_loop(full, 1024 // vc, open_step, 0)
         for h in range(HEADS):
-            top, total, expect = state[h]
+            part_m = run_m[h]
+            top = jnp.max(part_m, axis=0, keepdims=True)
+            weight = jnp.exp(part_m - top)
+            total = jnp.sum(run_t[h] * weight, axis=0, keepdims=True)
+            expect = jnp.sum(run_e[h] * weight, axis=0, keepdims=True)
             some = total > 0.0
             safe = jnp.where(some, total, 1.0)
             log = jnp.where(some, top + jnp.log(safe), NEG)
             mean = expect / safe
-            for t in range(UB // 128):
-                out[2 * i + t, h : h + 1, :] = log[:, t * 128 : (t + 1) * 128]
-                out[2 * i + t, HEADS + h : HEADS + h + 1, :] = mean[:, t * 128 : (t + 1) * 128]
+            for t in range(ub // 128):
+                at = i * (ub // 128) + t
+                out[at, h : h + 1, :] = log[:, t * 128 : (t + 1) * 128]
+                out[at, HEADS + h : HEADS + h + 1, :] = mean[:, t * 128 : (t + 1) * 128]
         return 0
 
-    lax.fori_loop(0, 2048 // UB, sources, 0)
-
-
-def stats(q, k, f, b, grains, pu):
+    lax.fori_loop(0, 2048 // ub, sources, 0)
+
+
+def stats(q, k, f, b, meta, pu):
+    bf = jnp.bfloat16
     return pl.pallas_call(
         stats_kernel,
         in_specs=[VM] * 4 + [SM, VM],
-        out_specs=VM,
-        out_shape=jax.ShapeDtypeStruct((16, 16, 128), jnp.float32),
+        out_specs=[VM] * 5,
+        out_shape=[
+            jax.ShapeDtypeStruct((16, 16, 128), jnp.float32),
+            jax.ShapeDtypeStruct((2048, 512), bf),
+            jax.ShapeDtypeStruct((1024, 512), bf),
+            jax.ShapeDtypeStruct((2048, 256), bf),
+            jax.ShapeDtypeStruct((1024, 256), bf),
+        ],
         scratch_shapes=[
-            pltpu.VMEM((HEADS, 1024, 128), jnp.bfloat16),
-            pltpu.VMEM((1024, 256), jnp.bfloat16),
-        ],
-        compiler_params=pltpu.CompilerParams(vmem_limit_bytes=40 << 20),
+            pltpu.VMEM((HEADS, 1024, 128), bf),
+            pltpu.VMEM((2048, 256), bf),
+            pltpu.VMEM((1024, 256), bf),
+            pltpu.VMEM((HEADS, 8, UB1), jnp.float32),
+            pltpu.VMEM((HEADS, 8, UB1), jnp.float32),
+            pltpu.VMEM((HEADS, 8, UB1), jnp.float32),
+        ],
+        compiler_params=pltpu.CompilerParams(vmem_limit_bytes=24 << 20),
         name="stats",
-    )(q, k, f, b, grains, pu)
-
-
-def grads_kernel(q_ref, k_ref, f_ref, b_ref, grains, pu_ref, st, qg, kg, km, kt, bt, qacc, kacc):
-    mask_keys(k_ref, km)
+    )(q, k, f, b, meta, pu)
+
+
+def grads_kernel(qs, ks, fs, bs, meta, pu_ref, st, qg, kg, km, kt, qacc, kacc):
+    ub, vc = UB2, VC2
+    mask_keys(ks, km)
     for block in range(8):
-        bt[block * 128 : (block + 1) * 128, :] = b_ref[block].T
-        kt[:, block * 128 : (block + 1) * 128] = k_ref[block].T
+        rows = slice(block * 128, (block + 1) * 128)
+        kt[:, rows] = ks[rows, :].T
     kacc[...] = jnp.zeros_like(kacc)
-    low = lax.broadcasted_iota(jnp.int32, (VC, 128), 1) < HEAD
+    low = lax.broadcasted_iota(jnp.int32, (vc, 128), 1) < HEAD
 
     def sources(i, _):
-        q = queries_of(i, q_ref)
-        both = jnp.concatenate([st[2 * i], st[2 * i + 1]], axis=1)
+        us = pl.ds(pl.multiple_of(i * ub, ub), ub)
+        first, full = chunk_bounds(meta, i, ub, vc)
+        both = jnp.concatenate([st[i * (ub // 128) + t] for t in range(ub // 128)], axis=1)
         qacc[...] = jnp.zeros_like(qacc)
 
-        def targets(j, _):
-            counts, valid = tile_terms(i, j, q_ref, f_ref, bt, grains, pu_ref)
-            vs = pl.multiple_of(j * VC, VC)
+        def targets(j, masked):
+            vs = pl.ds(pl.multiple_of(j * vc, vc), vc)
+            counts = nt(bs[vs, :], fs[us, :])
+            if masked:
+                valid = chunk_valid(meta, pu_ref[pl.ds(i, 1), :], j, ub, vc)
             pair = []
             for h in range(HEADS):
-                qp = q[:, (h // 2) * 128 : (h // 2 + 1) * 128]
-                s = nt(km[h, pl.ds(vs, VC), :], qp)
-                w = jnp.exp(jnp.where(valid, s - both[h : h + 1], NEG))
-                g = (w * (both[HEADS + h : HEADS + h + 1] - counts)).astype(jnp.bfloat16)
+                qp = qs[us, (h // 2) * 128 : (h // 2 + 1) * 128]
+                s = nt(km[h, vs, :], qp) - both[h : h + 1]
+                if masked:
+                    s = jnp.where(valid, s, NEG)
+                g = (jnp.exp(s) * (both[HEADS + h : HEADS + h + 1] - counts)).astype(jnp.bfloat16)
                 hs = slice(h * HEAD, (h + 1) * HEAD)
-                qacc[hs, :] += nn(kt[hs, pl.ds(vs, VC)], g)
+                qacc[hs, :] += nn(kt[hs, vs], g)
                 pair.append(nn(g, qp))
                 if h % 2:
                     cols = slice((h // 2) * 128, (h // 2 + 1) * 128)
-                    kacc[pl.ds(vs, VC), cols] += jnp.where(low, pair[-2], pair[-1])
+                    kacc[vs, cols] += jnp.where(low, pair[-2], pair[-1])
+
+        def masked_step(j, _):
+            targets(j, True)
             return 0
 
-        lax.fori_loop(0, 1024 // VC, targets, 0)
+        def open_step(j, _):
+            targets(j, False)
+            return 0
+
+        lax.fori_loop(first, full, masked_step, 0)
+        lax.fori_loop(full, 1024 // vc, open_step, 0)
         turned = (qacc[...] * SCALE).T.astype(jnp.bfloat16)
-        for t in range(UB // 128):
-            qg[2 * i + t] = turned[t * 128 : (t + 1) * 128]
+        for t in range(ub // GRAIN):
+            to = order_of(meta, 0, i * (ub // GRAIN) + t)
+            qg[rows_of(to), :] = turned[t * GRAIN : (t + 1) * GRAIN]
         return 0
 
-    lax.fori_loop(0, 2048 // UB, sources, 0)
-    for block in range(8):
-        kg[block] = kacc[block * 128 : (block + 1) * 128, :].astype(jnp.bfloat16)
-
-
-def grads(q, k, f, b, grains, pu, st):
+    lax.fori_loop(0, 2048 // ub, sources, 0)
+
+    def unsort(g, _):
+        kg[rows_of(order_of(meta, 1, g)), :] = kacc[rows_of(g), :].astype(jnp.bfloat16)
+        return 0
+
+    lax.fori_loop(0, NV, unsort, 0)
+
+
+def grads(qs, ks, fs, bs, meta, pu, st):
     bf = jnp.bfloat16
     return pl.pallas_call(
         grads_kernel,
         in_specs=[VM] * 4 + [SM, VM, VM],
         out_specs=[VM] * 2,
         out_shape=[
-            jax.ShapeDtypeStruct((16, 128, 512), bf),
-            jax.ShapeDtypeStruct((8, 128, 512), bf),
+            jax.ShapeDtypeStruct((2048, 512), bf),
+            jax.ShapeDtypeStruct((1024, 512), bf),
         ],
         scratch_shapes=[
             pltpu.VMEM((HEADS, 1024, 128), bf),
             pltpu.VMEM((512, 1024), bf),
-            pltpu.VMEM((1024, 256), bf),
-            pltpu.VMEM((512, UB), jnp.float32),
+            pltpu.VMEM((512, UB2), jnp.float32),
             pltpu.VMEM((1024, 512), jnp.float32),
         ],
-        compiler_params=pltpu.CompilerParams(vmem_limit_bytes=40 << 20),
+        compiler_params=pltpu.CompilerParams(vmem_limit_bytes=24 << 20),
         name="grads",
-    )(q, k, f, b, grains, pu, st)
+    )(qs, ks, fs, bs, meta, pu, st)
+
+
+def in_order(places):
+    n = places.shape[0]
+    rank = jnp.sum((places[None, :] < places[:, None]).astype(jnp.int32), axis=1)
+    index = jnp.arange(n, dtype=jnp.int32)
+    hit = rank[None, :] == index[:, None]
+    return (
+        jnp.sum(jnp.where(hit, index[None, :], 0), axis=1),
+        jnp.sum(jnp.where(hit, places[None, :], 0), axis=1),
+    )
 
 
 def local(queries, keys, fwd_table, bwd_table, step_weight, block_order):
@@ -531,13 +616,21 @@
     grid = block_order.reshape(8, 16, 4)
     line = lax.dynamic_index_in_dim(grid, row_id, 0, keepdims=False).reshape(64)
     column = lax.dynamic_index_in_dim(grid, col_id, 1, keepdims=False).reshape(32)
+    order_u, place_u = in_order(line)
+    order_v, place_v = in_order(column)
+    meta = jnp.concatenate([order_u, order_v, place_u, place_v])
     offsets = jnp.arange(GRAIN, dtype=jnp.int32)
-    pu = (line[:, None] * GRAIN + offsets[None, :]).reshape(2048 // UB, UB)
+    pu = (place_u[:, None] * GRAIN + offsets[None, :]).reshape(8, 256)
     q, k, f, b = gather(queries, keys, sf, sb)
-    f = f.reshape(16, 256, 128)
-    b = b.reshape(8, 256, 128)
-    merged = merge(stats(q, k, f, b, column, pu))
-    qg, kg = grads(q, k, f, b, column, pu, merged)
+    part, qs, ks, fs, bs = stats(
+        q.reshape(2048, 512),
+        k.reshape(1024, 512),
+        f.reshape(16, 256, 128),
+        b.reshape(8, 256, 128),
+        meta,
+        pu,
+    )
+    qg, kg = grads(qs, ks, fs, bs, meta, pu, merge(part))
     return reduce(qg.reshape(4, 2, 2, 128, 512), kg.reshape(2, 4, 128, 512))
 
 

time: 184 us -> 163 us (0.89)
  Pallas kernels: 171 us -> 155 us
  local copies, waits for them, and re-layouts: 10.8 us -> 5.36 us
    pallas_call x1, Pallas kernels: 38.8 us -> 21.7 us  [stats(): pl.pallas_call(stats_kernel, in_specs=[VM] * 4 + [SM, VM], out_specs=[VM]...]
    pallas_call x1, Pallas kernels: 23.8 us -> 33.7 us  [reduce(): pl.pallas_call(reduce_kernel, in_specs=[VM] * 2, out_specs=[VM] * 2, out_...]
    pallas_call x1, Pallas kernels: 59.2 us -> 50.3 us  [grads(): pl.pallas_call(grads_kernel, in_specs=[VM] * 4 + [SM, VM, VM], out_specs=...]
    unnamed x20 -> x8, local copies, waits for them, and re-layouts: 9.64 us -> 4.05 us
where the time goes in v2:
time: 163 us
  Pallas kernels  155 us (95%)
  local copies, waits for them, and re-layouts  5.36 us (3%)
  other arithmetic  1.64 us (1%)
    pallas_call x1, Pallas kernels, grads(): pl.pallas_call(grads_kernel, in_specs=[VM] * 4 + [SM, VM, VM], out_specs=...  50.3 us
    pallas_call x1, Pallas kernels, reduce(): pl.pallas_call(reduce_kernel, in_specs=[VM] * 2, out_specs=[VM] * 2, out_...  33.7 us
    pallas_call x1, Pallas kernels, gather(): pl.pallas_call(gather_kernel, in_specs=[VM] * 4, out_specs=[VM] * 4, out_...  33.6 us
    pallas_call x1, Pallas kernels, stats(): pl.pallas_call(stats_kernel, in_specs=[VM] * 4 + [SM, VM], out_specs=[VM]...  21.7 us
    pallas_call x1, Pallas kernels, merge(): pl.pallas_call(merge_kernel, in_specs=[VM], out_specs=VM, out_shape=jax.S...  16.1 us
    unnamed x8, local copies, waits for them, and re-layouts  4.05 us

profile of v2, /device:TPU:1, one launch (start us, length us, event | category | flops | bytes accessed | tf_op | source)
XLA Modules:
  0.0 163.2 jit_solution(9773111500810512982)
XLA Ops:
  0.6 0.1 add.33
  0.7 0.8 reshape.60
  1.6 0.1 lt.39
  1.7 0.1 lt.44
  1.7 0.2 convert_reduce_fusion.1
  1.9 0.1 select_reduce_fusion.3
  2.0 0.2 convert_reduce_fusion
  2.2 0.1 select_reduce_fusion.1
  2.3 0.1 pad_add_fusion.meta
  2.4 0.1 mul.26
  2.5 0.1 add.30
  2.6 0.1 add.31
  2.7 1.0 multiply_convert_fusion
  3.6 0.0 copy-start
  3.7 0.9 copy-done
  4.5 0.0 copy-start.1
  4.6 0.9 copy-done.1
  5.5 0.0 copy-start.2
  5.5 0.8 copy-done.2
  6.3 33.6 %gather.1 = (bf16[16,128,512]{2,1,0:T(8,128)(2,1)S(1)}, bf16[8,128,512]{2,1,0:T(8,128)(2,1)S(1)}, bf16[16,16,8,2,128]{4,3,2,1,0:T(2,128)(2,1)S(1)}, bf16[8,16,8,2,128]{4,3,2,1,0:T(2,128)(2,1)S(1)}) custom-call(bf16[128,512]{1,0:T(8,128)(2,1)S(1)} %copy-done, bf16[128,512]{1,0:T(8,128)(2,1)S(1)} %copy-done.1, bf16[8,16,2,128]{3,2,1,0:T(2,128)(2,1)S(1)} %bitcast.19, ...), custom_call_target="tpu_custom_call" | custom-call | tf_op jit(solution)/shard_map/gather/pallas_call | solution.py:208
  39.9 21.7 %stats.1 = (f32[16,16,128]{2,1,0:T(8,128)S(1)}, bf16[2048,512]{1,0:T(8,128)(2,1)S(1)}, bf16[1024,512]{1,0:T(8,128)(2,1)S(1)}, bf16[2048,256]{1,0:T(8,128)(2,1)S(1)}, bf16[1024,256]{1,0:T(8,128)(2,1)S(1)}) custom-call(bf16[2048,512]{1,0:T(8,128)(2,1)S(1)} %bitcast.13, bf16[1024,512]{1,0:T(8,128)(2,1)S(1)} %bitcast.15, bf16[16,256,128]{2,1,0:T(8,128)(2,1)S(1)} %bitcast.16, ...), custom_call_target="tpu_custom_call" | custom-call | tf_op jit(solution)/shard_map/stats/pallas_call | solution.py:495
  61.7 16.1 %merge.1.st = f32[16,16,128]{2,1,0:T(8,128)S(1)} custom-call(f32[16,16,128]{2,1,0:T(8,128)S(1)} %get-tuple-element.21.part), custom_call_target="tpu_custom_call" | custom-call | tf_op jit(solution)/shard_map/merge/pallas_call | solution.py:267
  77.8 50.3 %grads.1 = (bf16[2048,512]{1,0:T(8,128)(2,1)S(1)}, bf16[1024,512]{1,0:T(8,128)(2,1)S(1)}) custom-call(bf16[2048,512]{1,0:T(8,128)(2,1)S(1)} %get-tuple-element.17.qs, bf16[1024,512]{1,0:T(8,128)(2,1)S(1)} %get-tuple-element.18.ks, bf16[2048,256]{1,0:T(8,128)(2,1)S(1)} %get-tuple-element.19.fs, bf16[1024,256]{1,0:T(8,128)(2,1)S(1)} %get-tuple-element.20.bs, ...), custom_call_target="tpu_custom_call" | custom-call | tf_op jit(solution)/shard_map/grads/pallas_call | solution.py:580
  128.0 33.7 %reduce.5 = (f32[128,512]{1,0:T(8,128)S(1)}, f32[128,512]{1,0:T(8,128)S(1)}) custom-call(bf16[4,2,2,128,512]{4,3,2,1,0:T(8,128)(2,1)S(1)} %bitcast.12, bf16[2,4,128,512]{3,2,1,0:T(8,128)(2,1)S(1)} %bitcast.14), custom_call_target="tpu_custom_call" | custom-call | tf_op jit(solution)/shard_map/reduce/pallas_call | solution.py:349
  161.8 0.7 copy.10
  162.5 0.7 copy.11
  (5 shorter events, 0.0 us)
Async XLA Ops:
  3.6 0.9 copy-start
  4.5 0.9 copy-start.1
  5.5 0.8 copy-start.2

commit v3 on v2

--- a/solution.py
+++ b/solution.py
@@ -14,8 +14,11 @@
 TOP = -1e29
 NU = 64
 NV = 32
-UB1, VC1 = 256, 128
-UB2, VC2 = 256, 128
+TILES = 64
+SLOTS = 4
+UB = 256
+VC = 128
+SUB = 128
 MESH = pl.DeviceIdType.MESH
 VM = pl.BlockSpec(memory_space=pltpu.VMEM)
 SM = pl.BlockSpec(memory_space=pltpu.SMEM)
@@ -392,10 +395,10 @@
     return pl.ds(pl.multiple_of(g * GRAIN, GRAIN), GRAIN)
 
 
-def chunk_bounds(meta, i, ub, vc):
-    low = place_of(meta, 0, i * (ub // GRAIN))
-    high = place_of(meta, 0, (i + 1) * (ub // GRAIN) - 1)
-    per = vc // GRAIN
+def chunk_bounds(meta, i):
+    low = place_of(meta, 0, i * (UB // GRAIN))
+    high = place_of(meta, 0, (i + 1) * (UB // GRAIN) - 1)
+    per = VC // GRAIN
     first = jnp.int32(0)
     full = jnp.int32(0)
     for j in range(NV // per):
@@ -404,17 +407,22 @@
     return first, full
 
 
-def chunk_valid(meta, pu, j, ub, vc):
-    off = lax.broadcasted_iota(jnp.int32, (GRAIN, ub), 0)
-    per = vc // GRAIN
+def chunk_valid(meta, pu, j):
+    off = lax.broadcasted_iota(jnp.int32, (GRAIN, UB), 0)
+    per = VC // GRAIN
     pv = jnp.concatenate(
         [off + GRAIN * place_of(meta, 1, j * per + t) for t in range(per)], axis=0
     )
     return pv >= pu
 
 
-def stats_kernel(q_ref, k_ref, f_ref, b_ref, meta, pu_ref, out, qs, ks, fs, bs, km, ft, bt, run_m, run_t, run_e):
-    ub, vc = UB1, VC1
+def stats_kernel(
+    q_ref, k_ref, f_ref, b_ref, meta, pu_ref, out, qs, ks, fs, bs, ws, ms, km, ft, bt, run_m, run_t, run_e, held, sem
+):
+    def flush(n):
+        slot = n % SLOTS
+        return pltpu.make_async_copy(held.at[slot], ws.at[n], sem.at[slot])
+
     for block in range(16):
         ft[block * 128 : (block + 1) * 128, :] = f_ref[block].T
     for block in range(8):
@@ -436,41 +444,62 @@
     lax.fori_loop(0, NV, sort_targets, 0)
     mask_keys(ks, km)
 
-    def sources(i, _):
-        us = pl.ds(pl.multiple_of(i * ub, ub), ub)
-        first, full = chunk_bounds(meta, i, ub, vc)
+    def sources(i, tile):
+        us = pl.ds(pl.multiple_of(i * UB, UB), UB)
+        first, full = chunk_bounds(meta, i)
+        full += full % 2
         run_m[...] = jnp.full_like(run_m, TOP)
         run_t[...] = jnp.zeros_like(run_t)
         run_e[...] = jnp.zeros_like(run_e)
 
-        def targets(j, masked):
-            vs = pl.ds(pl.multiple_of(j * vc, vc), vc)
-            counts = nt(bs[vs, :], fs[us, :]).reshape(vc // 8, 8, ub)
+        def targets(j, width, masked):
+            rows = width * VC
+            vs = pl.ds(pl.multiple_of(j * VC, VC), rows)
+            n = tile + j - first
+            for t in range(width):
+
+                @pl.when(n + t >= SLOTS)
+                def _():
+                    flush(n + t - SLOTS).wait()
+
+            counts = nt(bs[vs, :], fs[us, :])
             if masked:
-                valid = chunk_valid(meta, pu_ref[pl.ds(i, 1), :], j, ub, vc)
+                valid = chunk_valid(meta, pu_ref[pl.ds(i, 1), :], j)
             for h in range(HEADS):
-                s = nt(km[h, vs, :], qs[us, (h // 2) * 128 : (h // 2 + 1) * 128])
+                scores = nt(km[h, vs, :], qs[us, (h // 2) * 128 : (h // 2 + 1) * 128])
                 if masked:
-                    s = jnp.where(valid, s, NEG)
-                s = s.reshape(vc // 8, 8, ub)
-                old = run_m[h]
-                new = jnp.maximum(old, jnp.max(s, axis=0))
-                w = jnp.exp(s - new[None])
-                shrink = jnp.exp(old - new)
-                run_m[h] = new
-                run_t[h] = run_t[h] * shrink + jnp.sum(w, axis=0)
-                run_e[h] = run_e[h] * shrink + jnp.sum(w * counts, axis=0)
+                    scores = jnp.where(valid, scores, NEG)
+                for t in range(rows // SUB):
+                    part = slice(t * SUB, (t + 1) * SUB)
+                    s = scores[part].reshape(SUB // 8, 8, UB)
+                    old = run_m[h]
+                    new = jnp.maximum(old, jnp.max(s, axis=0))
+                    w = jnp.exp(s - new[None])
+                    shrink = jnp.exp(old - new)
+                    run_m[h] = new
+                    run_t[h] = run_t[h] * shrink + jnp.sum(w, axis=0)
+                    run_e[h] = run_e[h] * shrink + jnp.sum(
+                        w * counts[part].reshape(SUB // 8, 8, UB), axis=0
+                    )
+                    at = t * SUB // VC
+                    inner = t % (VC // SUB)
+                    held[(n + at) % SLOTS, h, inner * SUB : (inner + 1) * SUB, :] = w.reshape(
+                        SUB, UB
+                    ).astype(jnp.bfloat16)
+                    ms[n + at, h, inner] = new
+            for t in range(width):
+                flush(n + t).start()
 
         def masked_step(j, _):
-            targets(j, True)
+            targets(j, 1, True)
             return 0
 
         def open_step(j, _):
-            targets(j, False)
+            targets(full + 2 * j, 2, False)
             return 0
 
         lax.fori_loop(first, full, masked_step, 0)
-        lax.fori_loop(full, 1024 // vc, open_step, 0)
+        lax.fori_loop(0, (1024 // VC - full) // 2, open_step, 0)
         for h in range(HEADS):
             part_m = run_m[h]
             top = jnp.max(part_m, axis=0, keepdims=True)
@@ -481,13 +510,18 @@
             safe = jnp.where(some, total, 1.0)
             log = jnp.where(some, top + jnp.log(safe), NEG)
             mean = expect / safe
-            for t in range(ub // 128):
-                at = i * (ub // 128) + t
+            for t in range(UB // 128):
+                at = i * (UB // 128) + t
                 out[at, h : h + 1, :] = log[:, t * 128 : (t + 1) * 128]
                 out[at, HEADS + h : HEADS + h + 1, :] = mean[:, t * 128 : (t + 1) * 128]
-        return 0
-
-    lax.fori_loop(0, 2048 // ub, sources, 0)
+        return tile + 1024 // VC - first
+
+    count = lax.fori_loop(0, 2048 // UB, sources, jnp.int32(0))
+    for back in range(1, SLOTS + 1):
+
+        @pl.when(count >= back)
+        def _():
+            flush(count - back).wait()
 
 
 def stats(q, k, f, b, meta, pu):
@@ -495,78 +529,111 @@
     return pl.pallas_call(
         stats_kernel,
         in_specs=[VM] * 4 + [SM, VM],
-        out_specs=[VM] * 5,
+        out_specs=[VM] * 5 + [pl.BlockSpec(memory_space=pl.ANY), VM],
         out_shape=[
             jax.ShapeDtypeStruct((16, 16, 128), jnp.float32),
             jax.ShapeDtypeStruct((2048, 512), bf),
             jax.ShapeDtypeStruct((1024, 512), bf),
             jax.ShapeDtypeStruct((2048, 256), bf),
             jax.ShapeDtypeStruct((1024, 256), bf),
+            jax.ShapeDtypeStruct((TILES, HEADS, VC, UB), bf),
+            jax.ShapeDtypeStruct((TILES, HEADS, VC // SUB, 8, UB), jnp.float32),
         ],
         scratch_shapes=[
             pltpu.VMEM((HEADS, 1024, 128), bf),
             pltpu.VMEM((2048, 256), bf),
             pltpu.VMEM((1024, 256), bf),
-            pltpu.VMEM((HEADS, 8, UB1), jnp.float32),
-            pltpu.VMEM((HEADS, 8, UB1), jnp.float32),
-            pltpu.VMEM((HEADS, 8, UB1), jnp.float32),
+            pltpu.VMEM((HEADS, 8, UB), jnp.float32),
+            pltpu.VMEM((HEADS, 8, UB), jnp.float32),
+            pltpu.VMEM((HEADS, 8, UB), jnp.float32),
+            pltpu.VMEM((SLOTS, HEADS, VC, UB), bf),
+            pltpu.SemaphoreType.DMA((SLOTS,)),
         ],
-        compiler_params=pltpu.CompilerParams(vmem_limit_bytes=24 << 20),
+        compiler_params=pltpu.CompilerParams(vmem_limit_bytes=12 << 20),
         name="stats",
     )(q, k, f, b, meta, pu)
 
 
-def grads_kernel(qs, ks, fs, bs, meta, pu_ref, st, qg, kg, km, kt, qacc, kacc):
-    ub, vc = UB2, VC2
-    mask_keys(ks, km)
+def grads_kernel(qs, ks, fs, bs, ws, ms, meta, st, qg, kg, kt, qacc, kacc, held, sem):
+    def fetch(n):
+        slot = n % SLOTS
+        return pltpu.make_async_copy(ws.at[n], held.at[slot], sem.at[slot])
+
+    count = jnp.int32(0)
+    for i in range(2048 // UB):
+        count += 1024 // VC - chunk_bounds(meta, i)[0]
+    for n in range(SLOTS):
+
+        @pl.when(count > n)
+        def _():
+            fetch(n).start()
+
     for block in range(8):
         rows = slice(block * 128, (block + 1) * 128)
         kt[:, rows] = ks[rows, :].T
     kacc[...] = jnp.zeros_like(kacc)
-    low = lax.broadcasted_iota(jnp.int32, (vc, 128), 1) < HEAD
-
-    def sources(i, _):
-        us = pl.ds(pl.multiple_of(i * ub, ub), ub)
-        first, full = chunk_bounds(meta, i, ub, vc)
-        both = jnp.concatenate([st[i * (ub // 128) + t] for t in range(ub // 128)], axis=1)
+
+    def sources(i, tile):
+        us = pl.ds(pl.multiple_of(i * UB, UB), UB)
+        first, _ = chunk_bounds(meta, i)
+        both = jnp.concatenate([st[i * (UB // 128) + t] for t in range(UB // 128)], axis=1)
         qacc[...] = jnp.zeros_like(qacc)
 
-        def targets(j, masked):
-            vs = pl.ds(pl.multiple_of(j * vc, vc), vc)
+        def targets(j, width):
+            rows = width * VC
+            vs = pl.ds(pl.multiple_of(j * VC, VC), rows)
+            n = tile + j - first
+            for t in range(width):
+                fetch(n + t).wait()
             counts = nt(bs[vs, :], fs[us, :])
-            if masked:
-                valid = chunk_valid(meta, pu_ref[pl.ds(i, 1), :], j, ub, vc)
+            low = lax.broadcasted_iota(jnp.int32, (rows, 128), 1) < HEAD
             pair = []
             for h in range(HEADS):
-                qp = qs[us, (h // 2) * 128 : (h // 2 + 1) * 128]
-                s = nt(km[h, vs, :], qp) - both[h : h + 1]
-                if masked:
-                    s = jnp.where(valid, s, NEG)
-                g = (jnp.exp(s) * (both[HEADS + h : HEADS + h + 1] - counts)).astype(jnp.bfloat16)
+                log = both[h : h + 1]
+                mean = both[HEADS + h : HEADS + h + 1]
+                parts = []
+                for t in range(rows // SUB):
+                    at = t * SUB // VC
+                    inner = t % (VC // SUB)
+                    part = slice(t * SUB, (t + 1) * SUB)
+                    w = held[(n + at) % SLOTS, h, inner * SUB : (inner + 1) * SUB, :].astype(
+                        jnp.float32
+                    )
+                    scale = jnp.exp(ms[n + at, h, inner] - log)
+                    w = (w.reshape(SUB // 8, 8, UB) * scale[None]).reshape(SUB, UB)
+                    parts.append((w * (mean - counts[part])).astype(jnp.bfloat16))
+                g = jnp.concatenate(parts, axis=0)
                 hs = slice(h * HEAD, (h + 1) * HEAD)
                 qacc[hs, :] += nn(kt[hs, vs], g)
-                pair.append(nn(g, qp))
+                pair.append(nn(g, qs[us, (h // 2) * 128 : (h // 2 + 1) * 128]))
                 if h % 2:
                     cols = slice((h // 2) * 128, (h // 2 + 1) * 128)
                     kacc[vs, cols] += jnp.where(low, pair[-2], pair[-1])
-
-        def masked_step(j, _):
-            targets(j, True)
+            for t in range(width):
+
+                @pl.when(n + t + SLOTS < count)
+                def _():
+                    fetch(n + t + SLOTS).start()
+
+        odd = first % 2
+
+        def single(j, _):
+            targets(first, 1)
             return 0
 
-        def open_step(j, _):
-            targets(j, False)
+        def double(j, _):
+            targets(first + odd + 2 * j, 2)
             return 0
 
-        lax.fori_loop(first, full, masked_step, 0)
-        lax.fori_loop(full, 1024 // vc, open_step, 0)
+        lax.fori_loop(0, odd, single, 0)
+        lax.fori_loop(0, (1024 // VC - first) // 2, double, 0)
         turned = (qacc[...] * SCALE).T.astype(jnp.bfloat16)
-        for t in range(ub // GRAIN):
-            to = order_of(meta, 0, i * (ub // GRAIN) + t)
+        for t in range(UB // GRAIN):
+            to = order_of(meta, 0, i * (UB // GRAIN) + t)
             qg[rows_of(to), :] = turned[t * GRAIN : (t + 1) * GRAIN]
-        return 0
-
-    lax.fori_loop(0, 2048 // ub, sources, 0)
+        return tile + 1024 // VC - first
+
+    lax.fori_loop(0, 2048 // UB, sources, jnp.int32(0))
 
     def unsort(g, _):
         kg[rows_of(order_of(meta, 1, g)), :] = kacc[rows_of(g), :].astype(jnp.bfloat16)
@@ -575,25 +642,26 @@
     lax.fori_loop(0, NV, unsort, 0)
 
 
-def grads(qs, ks, fs, bs, meta, pu, st):
+def grads(qs, ks, fs, bs, ws, ms, meta, st):
     bf = jnp.bfloat16
     return pl.pallas_call(
         grads_kernel,
-        in_specs=[VM] * 4 + [SM, VM, VM],
+        in_specs=[VM] * 4 + [pl.BlockSpec(memory_space=pl.ANY), VM, SM, VM],
         out_specs=[VM] * 2,
         out_shape=[
             jax.ShapeDtypeStruct((2048, 512), bf),
             jax.ShapeDtypeStruct((1024, 512), bf),
         ],
         scratch_shapes=[
-            pltpu.VMEM((HEADS, 1024, 128), bf),
             pltpu.VMEM((512, 1024), bf),
-            pltpu.VMEM((512, UB2), jnp.float32),
+            pltpu.VMEM((512, UB), jnp.float32),
             pltpu.VMEM((1024, 512), jnp.float32),
+            pltpu.VMEM((SLOTS, HEADS, VC, UB), bf),
+            pltpu.SemaphoreType.DMA((SLOTS,)),
         ],
-        compiler_params=pltpu.CompilerParams(vmem_limit_bytes=24 << 20),
+        compiler_params=pltpu.CompilerParams(vmem_limit_bytes=12 << 20),
         name="grads",
-    )(qs, ks, fs, bs, meta, pu, st)
+    )(qs, ks, fs, bs, ws, ms, meta, st)
 
 
 def in_order(places):
@@ -622,7 +690,7 @@
     offsets = jnp.arange(GRAIN, dtype=jnp.int32)
     pu = (place_u[:, None] * GRAIN + offsets[None, :]).reshape(8, 256)
     q, k, f, b = gather(queries, keys, sf, sb)
-    part, qs, ks, fs, bs = stats(
+    part, qs, ks, fs, bs, ws, ms = stats(
         q.reshape(2048, 512),
         k.reshape(1024, 512),
         f.reshape(16, 256, 128),
@@ -630,7 +698,7 @@
         meta,
         pu,
     )
-    qg, kg = grads(qs, ks, fs, bs, meta, pu, merge(part))
+    qg, kg = grads(qs, ks, fs, bs, ws, ms, meta, merge(part))
     return reduce(qg.reshape(4, 2, 2, 128, 512), kg.reshape(2, 4, 128, 512))
 
 

time: 163 us -> 130 us (0.80)
  Pallas kernels: 155 us -> 121 us
    pallas_call x1, Pallas kernels: 50.3 us -> 24.5 us  [grads(): pl.pallas_call(grads_kernel, in_specs=[VM] * 4 + [pl.BlockSpec(memory_spa...]
    pallas_call x1, Pallas kernels: 33.7 us -> 23.6 us  [reduce(): pl.pallas_call(reduce_kernel, in_specs=[VM] * 2, out_specs=[VM] * 2, out_...]
    pallas_call x1, Pallas kernels: 21.7 us -> 24.5 us  [stats(): pl.pallas_call(stats_kernel, in_specs=[VM] * 4 + [SM, VM], out_specs=[VM]...]
where the time goes in v3:
time: 130 us; the launch traced here: 129 us
  Pallas kernels  121 us (93%)
  local copies, waits for them, and re-layouts  5.36 us (4%)
  other arithmetic  1.64 us (1%)
    pallas_call x1, Pallas kernels, gather(): pl.pallas_call(gather_kernel, in_specs=[VM] * 4, out_specs=[VM] * 4, out_...  33.6 us
    pallas_call x1, Pallas kernels, stats(): pl.pallas_call(stats_kernel, in_specs=[VM] * 4 + [SM, VM], out_specs=[VM]...  24.5 us
    pallas_call x1, Pallas kernels, grads(): pl.pallas_call(grads_kernel, in_specs=[VM] * 4 + [pl.BlockSpec(memory_spa...  24.5 us
    pallas_call x1, Pallas kernels, reduce(): pl.pallas_call(reduce_kernel, in_specs=[VM] * 2, out_specs=[VM] * 2, out_...  23.6 us
    pallas_call x1, Pallas kernels, merge(): pl.pallas_call(merge_kernel, in_specs=[VM], out_specs=VM, out_shape=jax.S...  14.8 us
    unnamed x8, local copies, waits for them, and re-layouts  4.05 us

profile of v3, /device:TPU:1, one launch (start us, length us, event | category | flops | bytes accessed | tf_op | source)
XLA Modules:
  0.0 128.7 jit_solution(3836672736157502084)
XLA Ops:
  0.6 0.1 add.33
  0.7 0.8 reshape.60
  1.6 0.1 lt.39
  1.7 0.1 lt.44
  1.7 0.2 convert_reduce_fusion.1
  1.9 0.1 select_reduce_fusion.3
  2.0 0.2 convert_reduce_fusion
  2.2 0.1 select_reduce_fusion.1
  2.3 0.1 pad_add_fusion.meta
  2.4 0.1 mul.26
  2.5 0.1 add.30
  2.6 0.1 add.31
  2.7 1.0 multiply_convert_fusion
  3.6 0.0 copy-start
  3.7 0.9 copy-done
  4.5 0.0 copy-start.1
  4.6 0.9 copy-done.1
  5.5 0.0 copy-start.2
  5.5 0.8 copy-done.2
  6.3 33.6 %gather.1 = (bf16[16,128,512]{2,1,0:T(8,128)(2,1)S(1)}, bf16[8,128,512]{2,1,0:T(8,128)(2,1)S(1)}, bf16[16,16,8,2,128]{4,3,2,1,0:T(2,128)(2,1)S(1)}, bf16[8,16,8,2,128]{4,3,2,1,0:T(2,128)(2,1)S(1)}) custom-call(bf16[128,512]{1,0:T(8,128)(2,1)S(1)} %copy-done, bf16[128,512]{1,0:T(8,128)(2,1)S(1)} %copy-done.1, bf16[8,16,2,128]{3,2,1,0:T(2,128)(2,1)S(1)} %bitcast.19, ...), custom_call_target="tpu_custom_call" | custom-call | tf_op jit(solution)/shard_map/gather/pallas_call | solution.py:211
  39.9 24.5 %stats.1 = (f32[16,16,128]{2,1,0:T(8,128)S(1)}, bf16[2048,512]{1,0:T(8,128)(2,1)S(1)}, bf16[1024,512]{1,0:T(8,128)(2,1)S(1)}, bf16[2048,256]{1,0:T(8,128)(2,1)S(...) custom-call(bf16[2048,512]{1,0:T(8,128)(2,1)S(1)} %bitcast.13, ...), custom_call_target="tpu_custom_call" | custom-call | tf_op jit(solution)/shard_map/stats/pallas_call | solution.py:529
  64.4 14.8 %merge.1.st = f32[16,16,128]{2,1,0:T(8,128)S(1)} custom-call(f32[16,16,128]{2,1,0:T(8,128)S(1)} %get-tuple-element.25.part), custom_call_target="tpu_custom_call" | custom-call | tf_op jit(solution)/shard_map/merge/pallas_call | solution.py:270
  79.2 24.5 %grads.1 = (bf16[2048,512]{1,0:T(8,128)(2,1)S(1)}, bf16[1024,512]{1,0:T(8,128)(2,1)S(1)}) custom-call(bf16[2048,512]{1,0:T(8,128)(2,1)S(1)} %get-tuple-element.19.qs, bf16[1024,512]{1,0:T(8,128)(2,1)S(1)} %get-tuple-element.20.ks, bf16[2048,256]{1,0:T(8,128)(2,1)S(1)} %get-tuple-element.21.fs, bf16[1024,256]{1,0:T(8,128)(2,1)S(1)} %get-tuple-element.22.bs, ...), custom_call_target="tpu_custom_call" | custom-call | tf_op jit(solution)/shard_map/grads/pallas_call | solution.py:647
  103.7 23.6 %reduce.5 = (f32[128,512]{1,0:T(8,128)S(1)}, f32[128,512]{1,0:T(8,128)S(1)}) custom-call(bf16[4,2,2,128,512]{4,3,2,1,0:T(8,128)(2,1)S(1)} %bitcast.12, bf16[2,4,128,512]{3,2,1,0:T(8,128)(2,1)S(1)} %bitcast.14), custom_call_target="tpu_custom_call" | custom-call | tf_op jit(solution)/shard_map/reduce/pallas_call | solution.py:352
  127.3 0.7 copy.10
  128.0 0.7 copy.11
  (5 shorter events, 0.0 us)
Async XLA Ops:
  3.6 0.9 copy-start
  4.5 0.9 copy-start.1
  5.5 0.8 copy-start.2
